TPU v7x, 128 devices: a whole 4x4x4 slice. The times are simulated.
128 devices in a mesh: section: 8 (over y_hi, z), seq: 16 (over x, y_lo, core).
Axes of the slice: x: 4, y: 4 (y_hi: 2, y_lo: 2; y = y_hi * 2 + y_lo), z: 4, core: 2. Of those that a mesh axis runs over, the one named last changes fastest.
Arguments:
- inbound_embedding_batches: bfloat16 [2, 128, 4096], replicated, may hold values from -16 to 16
- decoder_embedding_batches: bfloat16 [2, 128, 4096], replicated, may hold values from -16 to 16
- asking_projections: bfloat16 [8, 4096, 4096], P('section', None, 'seq'), may hold values from -0.09375 to 0.09375
- probe_projections: bfloat16 [8, 4096, 4096], P('section', None, 'seq'), may hold values from -0.09375 to 0.09375
- payload_projections: bfloat16 [8, 4096, 4096], P('section', None, 'seq'), may hold values from -0.09375 to 0.09375
- exit_projections: bfloat16 [8, 4096, 4096], P('section', 'seq'), may hold values from -0.1875 to 0.1875
- layer_rescale_weights: float32 [8, 4096], P('section'), may hold values from 0.1 to 1.9
- logit_sharpness: float32 [8, 64], P('section', 'seq'), may hold values from 0.5 to 3
- last_rescale_weights: float32 [4096], replicated, may hold values from 0.1 to 1.9
Outputs:
- section_out: bfloat16 [8, 2, 128, 4096], P('section')
All inputs are finite; a program needn't handle non-finite values.
Results may differ from a plain program's by a relative error of at most 0.025.
Values may be sent and summed in bfloat16 or wider, within the bound.
A program may use at most 64 MiB of HBM per device.

v0:
```python
import math

import jax
import jax.numpy as jnp
from jax import lax
from jax.sharding import PartitionSpec as P

epsilon = 1e-06


def from_behind(x, axis, by):
    count = lax.axis_size(axis)
    pairs = [(i, i + by) for i in range(count) if 0 <= i + by < count]
    return lax.ppermute(x, axis, pairs)


def broadcast(value, axis, source):
    kept = jnp.where(lax.axis_index(axis) == source, value, 0).astype(value.dtype)
    return lax.psum(kept, axis)


def normalize(row_block, gain_vector):
    values = row_block.astype(jnp.float32)
    factor = lax.rsqrt(jnp.mean(values * values, axis=-1, keepdims=True) + epsilon)
    return (values * factor * gain_vector).astype(jnp.bfloat16)


def unit_heads(projected):
    return (
        projected * lax.rsqrt(jnp.mean(projected * projected, axis=-1, keepdims=True) + epsilon)
    ).astype(jnp.bfloat16)


def attend(queries, keys_proj, values_proj, logit_divisor):
    length = queries.shape[0]
    key_length = keys_proj.shape[0]
    head_count = logit_divisor.shape[0]
    head_size = queries.shape[1] // head_count
    unit_query = unit_heads(queries.reshape(length, head_count, head_size))
    unit_key = unit_heads(keys_proj.reshape(key_length, head_count, head_size))
    values = values_proj.astype(jnp.bfloat16).reshape(key_length, head_count, head_size)
    scores = jnp.einsum("qhd,khd->hqk", unit_query, unit_key, preferred_element_type=jnp.float32)
    scores = scores * (logit_divisor[:, None, None] / math.sqrt(head_size))
    weights = jnp.exp(scores)
    weights = (weights / jnp.sum(weights, axis=-1, keepdims=True)).astype(jnp.bfloat16)
    blended_payloads = jnp.einsum(
        "hqk,khd->qhd", weights, values, preferred_element_type=jnp.float32
    )
    return blended_payloads.astype(jnp.bfloat16).reshape(length, head_count * head_size)


def shards(
    inbound_embedding_batches,
    decoder_embedding_batches,
    asking_projections,
    probe_projections,
    payload_projections,
    exit_projections,
    layer_rescale_weights,
    logit_sharpness,
    last_rescale_weights,
):
    section_count = lax.axis_size("section")
    seq_count = lax.axis_size("seq")
    present_layer_index = lax.axis_index("section")
    seq_index = lax.axis_index("seq")
    encoders = 3 * section_count // 8
    batches = inbound_embedding_batches.shape[0]
    length = inbound_embedding_batches.shape[1]
    width = inbound_embedding_batches.shape[2]
    share_rows = length // seq_count
    first_own = seq_index * share_rows
    ticks = section_count + batches - 1
    w_query = asking_projections[0]
    w_key = probe_projections[0]
    w_value = payload_projections[0]
    w_output = exit_projections[0]
    logit_divisor = logit_sharpness[0]
    gain_vector = layer_rescale_weights[0]
    is_encoder = present_layer_index < encoders

    def layer(stream, memory_raw):
        rescaled_activations = normalize(stream, gain_vector)
        remote = normalize(memory_raw, last_rescale_weights)
        source_kv = jnp.where(is_encoder, rescaled_activations, remote)
        queries = jnp.dot(rescaled_activations, w_query, preferred_element_type=jnp.float32)
        keys_proj = jnp.dot(source_kv, w_key, preferred_element_type=jnp.float32)
        values_proj = jnp.dot(source_kv, w_value, preferred_element_type=jnp.float32)
        blended_payloads = attend(queries, keys_proj, values_proj, logit_divisor)
        update = lax.psum_scatter(
            jnp.dot(blended_payloads, w_output, preferred_element_type=jnp.float32).astype(
                jnp.bfloat16
            ),
            "seq",
            scatter_dimension=0,
            tiled=True,
        ).astype(jnp.float32)
        own_rows = lax.dynamic_slice_in_dim(stream, first_own, share_rows, 0)
        return (own_rows.astype(jnp.float32) + update).astype(jnp.bfloat16)

    blank = jnp.zeros((length, width), inbound_embedding_batches.dtype)
    holder = jnp.zeros((batches,) + blank.shape, inbound_embedding_batches.dtype)

    def advance(tick_index, state_tuple):
        arrived, carried, stored, finished = state_tuple
        offset = tick_index - present_layer_index
        batch_index = jnp.clip(offset, 0, batches - 1)
        valid = (offset >= 0) & (offset < batches)
        source_rows = lax.dynamic_index_in_dim(
            inbound_embedding_batches, batch_index, 0, keepdims=False
        )
        target_rows = lax.dynamic_index_in_dim(
            decoder_embedding_batches, batch_index, 0, keepdims=False
        )
        memory_kept = lax.dynamic_index_in_dim(stored, batch_index, 0, keepdims=False)
        arrived_rows = arrived
        stream = jnp.where(
            present_layer_index == 0,
            source_rows,
            jnp.where(present_layer_index == encoders, target_rows, arrived_rows),
        )
        share = layer(stream, memory_kept)
        outgoing = lax.all_gather(share, "seq", axis=0, tiled=True)
        written = lax.dynamic_update_index_in_dim(finished, outgoing, batch_index, 0)
        finished = jnp.where(valid, written, finished)
        arrived = from_behind(outgoing, "section", 1)
        encoded = broadcast(outgoing, "section", encoders - 1)
        produced = tick_index - (encoders - 1)
        ready = (produced >= 0) & (produced < batches)
        placed = lax.dynamic_update_index_in_dim(
            stored, encoded, jnp.clip(produced, 0, batches - 1), 0
        )
        stored = jnp.where(ready, placed, stored)
        return (arrived, carried, stored, finished)

    final_state = lax.fori_loop(0, ticks, advance, (blank, blank, holder, holder))
    finished = final_state[3]
    return finished[None]


def solution(mesh):
    return jax.shard_map(
        shards,
        mesh=mesh,
        in_specs=(
            P(),
            P(),
            P("section", None, "seq"),
            P("section", None, "seq"),
            P("section", None, "seq"),
            P("section", "seq", None),
            P("section", None),
            P("section", "seq"),
            P(),
        ),
        out_specs=P("section", None, None, None),
        check_vma=False,
    )
```

profile of v0, /device:TPU:123, one launch (start us, length us, event | category | flops | bytes accessed | tf_op | source)
XLA Modules:
  0.0 1815.6 jit_solution(14866793786622618340)
XLA Ops:
  9.4 1799.3 %while.19 = (s32[]{:T(128)}, bf16[128,4096]{1,0:T(8,128)(2,1)}, bf16[2,128,4096]{2,1,0:T(8,128)(2,1)S(1)}, bf16[2,128,4096]{2,1,0:T(8,128)(2,1)}, pred[]{:T(512)...) while((s32[]{:T(128)}, bf16[128,4096]{1,0:T(8,128)(2,1)}, ...), condition=%wide.region_8.9_spmd, body=%wide.region_0.8_spmd.sunk | while | flops 1104807808 | bytes 77665632 | solution.py:136
  10.1 2.8 fusion.48
  13.0 1.7 multiply_reduce_fusion.4
  21.4 3.0 convolution_convert_fusion.8
  24.5 54.0 %reduce-scatter.2.cloned.1.call-done = bf16[8,4096]{1,0:T(8,128)(2,1)} async-done(((bf16[128,4096]{1,0:T(8,128)(2,1)}), bf16[8,4096]{1,0:T(8,128)(2,1)}) %reduce-scatter.2.cloned.1.call-update) | async-done | bytes 65552 | tf_op jit(solution)/shard_map/while/body/eval_jaxpr/reduce_scatter | solution.py:90
  80.0 39.6 %all-gather.2.cloned.1.call-done = bf16[128,4096]{1,0:T(8,128)(2,1)} async-done(((bf16[8,4096]{1,0:T(8,128)(2,1)}), bf16[128,4096]{1,0:T(8,128)(2,1)}) %all-gather.2.cloned.1.call-update) | async-done | bytes 1048592 | tf_op jit(solution)/shard_map/while/body/eval_jaxpr/all_gather | solution.py:123
  122.5 2.4 fusion.51
  125.0 78.7 %all-reduce.2.cloned.1.call-done = bf16[1,128,4096]{2,1,0:T(8,128)(2,1)} async-done(((bf16[1,128,4096]{2,1,0:T(8,128)(2,1)}), bf16[1,128,4096]{2,1,0:T(8,128)(2,1)}) %all-reduce.2.cloned.1.call-update) | async-done | bytes 1048592 | tf_op jit(solution)/shard_map/while/body/eval_jaxpr/psum | solution.py:19
  204.7 2.8 fusion.48
  207.5 1.7 multiply_reduce_fusion.4
  216.0 3.0 convolution_convert_fusion.8
  219.1 59.7 %reduce-scatter.2.cloned.1.call-done = bf16[8,4096]{1,0:T(8,128)(2,1)} async-done(((bf16[128,4096]{1,0:T(8,128)(2,1)}), bf16[8,4096]{1,0:T(8,128)(2,1)}) %reduce-scatter.2.cloned.1.call-update) | async-done | bytes 65552 | tf_op jit(solution)/shard_map/while/body/eval_jaxpr/reduce_scatter | solution.py:90
  280.3 39.6 %all-gather.2.cloned.1.call-done = bf16[128,4096]{1,0:T(8,128)(2,1)} async-done(((bf16[8,4096]{1,0:T(8,128)(2,1)}), bf16[128,4096]{1,0:T(8,128)(2,1)}) %all-gather.2.cloned.1.call-update) | async-done | bytes 1048592 | tf_op jit(solution)/shard_map/while/body/eval_jaxpr/all_gather | solution.py:123
  322.8 2.4 fusion.51
  325.3 78.6 %all-reduce.2.cloned.1.call-done = bf16[1,128,4096]{2,1,0:T(8,128)(2,1)} async-done(((bf16[1,128,4096]{2,1,0:T(8,128)(2,1)}), bf16[1,128,4096]{2,1,0:T(8,128)(2,1)}) %all-reduce.2.cloned.1.call-update) | async-done | bytes 1048592 | tf_op jit(solution)/shard_map/while/body/eval_jaxpr/psum | solution.py:19
  404.8 2.8 fusion.48
  407.7 1.7 multiply_reduce_fusion.4
  416.1 3.0 convolution_convert_fusion.8
  419.3 59.7 %reduce-scatter.2.cloned.1.call-done = bf16[8,4096]{1,0:T(8,128)(2,1)} async-done(((bf16[128,4096]{1,0:T(8,128)(2,1)}), bf16[8,4096]{1,0:T(8,128)(2,1)}) %reduce-scatter.2.cloned.1.call-update) | async-done | bytes 65552 | tf_op jit(solution)/shard_map/while/body/eval_jaxpr/reduce_scatter | solution.py:90
  480.5 39.8 %all-gather.2.cloned.1.call-done = bf16[128,4096]{1,0:T(8,128)(2,1)} async-done(((bf16[8,4096]{1,0:T(8,128)(2,1)}), bf16[128,4096]{1,0:T(8,128)(2,1)}) %all-gather.2.cloned.1.call-update) | async-done | bytes 1048592 | tf_op jit(solution)/shard_map/while/body/eval_jaxpr/all_gather | solution.py:123
  523.2 2.4 fusion.51
  525.6 78.6 %all-reduce.2.cloned.1.call-done = bf16[1,128,4096]{2,1,0:T(8,128)(2,1)} async-done(((bf16[1,128,4096]{2,1,0:T(8,128)(2,1)}), bf16[1,128,4096]{2,1,0:T(8,128)(2,1)}) %all-reduce.2.cloned.1.call-update) | async-done | bytes 1048592 | tf_op jit(solution)/shard_map/while/body/eval_jaxpr/psum | solution.py:19
  606.5 2.8 fusion.48
  609.3 1.7 multiply_reduce_fusion.4
  617.8 3.0 convolution_convert_fusion.8
  620.9 59.2 %reduce-scatter.2.cloned.1.call-done = bf16[8,4096]{1,0:T(8,128)(2,1)} async-done(((bf16[128,4096]{1,0:T(8,128)(2,1)}), bf16[8,4096]{1,0:T(8,128)(2,1)}) %reduce-scatter.2.cloned.1.call-update) | async-done | bytes 65552 | tf_op jit(solution)/shard_map/while/body/eval_jaxpr/reduce_scatter | solution.py:90
  681.7 40.3 %all-gather.2.cloned.1.call-done = bf16[128,4096]{1,0:T(8,128)(2,1)} async-done(((bf16[8,4096]{1,0:T(8,128)(2,1)}), bf16[128,4096]{1,0:T(8,128)(2,1)}) %all-gather.2.cloned.1.call-update) | async-done | bytes 1048592 | tf_op jit(solution)/shard_map/while/body/eval_jaxpr/all_gather | solution.py:123
  724.9 2.4 fusion.51
  727.3 78.6 %all-reduce.2.cloned.1.call-done = bf16[1,128,4096]{2,1,0:T(8,128)(2,1)} async-done(((bf16[1,128,4096]{2,1,0:T(8,128)(2,1)}), bf16[1,128,4096]{2,1,0:T(8,128)(2,1)}) %all-reduce.2.cloned.1.call-update) | async-done | bytes 1048592 | tf_op jit(solution)/shard_map/while/body/eval_jaxpr/psum | solution.py:19
  808.1 2.8 fusion.48
  811.0 1.7 multiply_reduce_fusion.4
  819.4 3.0 convolution_convert_fusion.8
  822.6 59.2 %reduce-scatter.2.cloned.1.call-done = bf16[8,4096]{1,0:T(8,128)(2,1)} async-done(((bf16[128,4096]{1,0:T(8,128)(2,1)}), bf16[8,4096]{1,0:T(8,128)(2,1)}) %reduce-scatter.2.cloned.1.call-update) | async-done | bytes 65552 | tf_op jit(solution)/shard_map/while/body/eval_jaxpr/reduce_scatter | solution.py:90
  883.4 40.0 %all-gather.2.cloned.1.call-done = bf16[128,4096]{1,0:T(8,128)(2,1)} async-done(((bf16[8,4096]{1,0:T(8,128)(2,1)}), bf16[128,4096]{1,0:T(8,128)(2,1)}) %all-gather.2.cloned.1.call-update) | async-done | bytes 1048592 | tf_op jit(solution)/shard_map/while/body/eval_jaxpr/all_gather | solution.py:123
  926.2 2.4 fusion.51
  928.7 78.5 %all-reduce.2.cloned.1.call-done = bf16[1,128,4096]{2,1,0:T(8,128)(2,1)} async-done(((bf16[1,128,4096]{2,1,0:T(8,128)(2,1)}), bf16[1,128,4096]{2,1,0:T(8,128)(2,1)}) %all-reduce.2.cloned.1.call-update) | async-done | bytes 1048592 | tf_op jit(solution)/shard_map/while/body/eval_jaxpr/psum | solution.py:19
  1008.2 2.8 fusion.48
  1011.1 1.7 multiply_reduce_fusion.4
  1019.5 3.0 convolution_convert_fusion.8
  1022.7 59.7 %reduce-scatter.2.cloned.1.call-done = bf16[8,4096]{1,0:T(8,128)(2,1)} async-done(((bf16[128,4096]{1,0:T(8,128)(2,1)}), bf16[8,4096]{1,0:T(8,128)(2,1)}) %reduce-scatter.2.cloned.1.call-update) | async-done | bytes 65552 | tf_op jit(solution)/shard_map/while/body/eval_jaxpr/reduce_scatter | solution.py:90
  1083.9 39.7 %all-gather.2.cloned.1.call-done = bf16[128,4096]{1,0:T(8,128)(2,1)} async-done(((bf16[8,4096]{1,0:T(8,128)(2,1)}), bf16[128,4096]{1,0:T(8,128)(2,1)}) %all-gather.2.cloned.1.call-update) | async-done | bytes 1048592 | tf_op jit(solution)/shard_map/while/body/eval_jaxpr/all_gather | solution.py:123
  1126.5 2.4 fusion.51
  1128.9 78.6 %all-reduce.2.cloned.1.call-done = bf16[1,128,4096]{2,1,0:T(8,128)(2,1)} async-done(((bf16[1,128,4096]{2,1,0:T(8,128)(2,1)}), bf16[1,128,4096]{2,1,0:T(8,128)(2,1)}) %all-reduce.2.cloned.1.call-update) | async-done | bytes 1048592 | tf_op jit(solution)/shard_map/while/body/eval_jaxpr/psum | solution.py:19
  1208.5 2.8 fusion.48
  1211.4 1.7 multiply_reduce_fusion.4
  1219.8 3.0 convolution_convert_fusion.8
  1222.9 59.7 %reduce-scatter.2.cloned.1.call-done = bf16[8,4096]{1,0:T(8,128)(2,1)} async-done(((bf16[128,4096]{1,0:T(8,128)(2,1)}), bf16[8,4096]{1,0:T(8,128)(2,1)}) %reduce-scatter.2.cloned.1.call-update) | async-done | bytes 65552 | tf_op jit(solution)/shard_map/while/body/eval_jaxpr/reduce_scatter | solution.py:90
  1284.2 39.7 %all-gather.2.cloned.1.call-done = bf16[128,4096]{1,0:T(8,128)(2,1)} async-done(((bf16[8,4096]{1,0:T(8,128)(2,1)}), bf16[128,4096]{1,0:T(8,128)(2,1)}) %all-gather.2.cloned.1.call-update) | async-done | bytes 1048592 | tf_op jit(solution)/shard_map/while/body/eval_jaxpr/all_gather | solution.py:123
  1326.8 2.4 fusion.51
  1329.2 78.6 %all-reduce.2.cloned.1.call-done = bf16[1,128,4096]{2,1,0:T(8,128)(2,1)} async-done(((bf16[1,128,4096]{2,1,0:T(8,128)(2,1)}), bf16[1,128,4096]{2,1,0:T(8,128)(2,1)}) %all-reduce.2.cloned.1.call-update) | async-done | bytes 1048592 | tf_op jit(solution)/shard_map/while/body/eval_jaxpr/psum | solution.py:19
  1408.8 2.8 fusion.48
  1411.7 1.7 multiply_reduce_fusion.4
  1420.2 3.0 convolution_convert_fusion.8
  1423.3 59.7 %reduce-scatter.2.cloned.1.call-done = bf16[8,4096]{1,0:T(8,128)(2,1)} async-done(((bf16[128,4096]{1,0:T(8,128)(2,1)}), bf16[8,4096]{1,0:T(8,128)(2,1)}) %reduce-scatter.2.cloned.1.call-update) | async-done | bytes 65552 | tf_op jit(solution)/shard_map/while/body/eval_jaxpr/reduce_scatter | solution.py:90
  1484.5 39.8 %all-gather.2.cloned.1.call-done = bf16[128,4096]{1,0:T(8,128)(2,1)} async-done(((bf16[8,4096]{1,0:T(8,128)(2,1)}), bf16[128,4096]{1,0:T(8,128)(2,1)}) %all-gather.2.cloned.1.call-update) | async-done | bytes 1048592 | tf_op jit(solution)/shard_map/while/body/eval_jaxpr/all_gather | solution.py:123
  1527.2 2.4 fusion.51
  1529.6 78.6 %all-reduce.2.cloned.1.call-done = bf16[1,128,4096]{2,1,0:T(8,128)(2,1)} async-done(((bf16[1,128,4096]{2,1,0:T(8,128)(2,1)}), bf16[1,128,4096]{2,1,0:T(8,128)(2,1)}) %all-reduce.2.cloned.1.call-update) | async-done | bytes 1048592 | tf_op jit(solution)/shard_map/while/body/eval_jaxpr/psum | solution.py:19
  1609.2 2.8 fusion.48
  1612.1 1.7 multiply_reduce_fusion.4
  1620.5 3.0 convolution_convert_fusion.8
  1623.7 59.8 %reduce-scatter.2.cloned.1.call-done = bf16[8,4096]{1,0:T(8,128)(2,1)} async-done(((bf16[128,4096]{1,0:T(8,128)(2,1)}), bf16[8,4096]{1,0:T(8,128)(2,1)}) %reduce-scatter.2.cloned.1.call-update) | async-done | bytes 65552 | tf_op jit(solution)/shard_map/while/body/eval_jaxpr/reduce_scatter | solution.py:90
  1685.0 39.5 %all-gather.2.cloned.1.call-done = bf16[128,4096]{1,0:T(8,128)(2,1)} async-done(((bf16[8,4096]{1,0:T(8,128)(2,1)}), bf16[128,4096]{1,0:T(8,128)(2,1)}) %all-gather.2.cloned.1.call-update) | async-done | bytes 1048592 | tf_op jit(solution)/shard_map/while/body/eval_jaxpr/all_gather | solution.py:123
  1727.4 2.4 fusion.51
  1729.9 78.5 %all-reduce.2.cloned.1.call-done = bf16[1,128,4096]{2,1,0:T(8,128)(2,1)} async-done(((bf16[1,128,4096]{2,1,0:T(8,128)(2,1)}), bf16[1,128,4096]{2,1,0:T(8,128)(2,1)}) %all-reduce.2.cloned.1.call-update) | async-done | bytes 1048592 | tf_op jit(solution)/shard_map/while/body/eval_jaxpr/psum | solution.py:19
  (315 shorter events, 114.6 us)
Async XLA Ops:
  7.6 1.8 copy-start.7
  9.5 69.0 %reduce-scatter.2.cloned.1.call-start = ((), (), s32[]{:S(2)}) async-start(), calls=%async_computation.1 | async-start | bytes 1114112 | tf_op jit(solution)/shard_map/while/body/eval_jaxpr/reduce_scatter | solution.py:90
  10.1 2.9 copy-start.6
  24.5 95.2 %all-gather.2.cloned.1.call-start = ((), (), s32[]{:S(2)}) async-start(), calls=%async_computation.2 | async-start | bytes 1114112 | tf_op jit(solution)/shard_map/while/body/eval_jaxpr/all_gather | solution.py:123
  80.0 123.7 %all-reduce.2.cloned.1.call-start = ((), (), s32[]{:S(2)}) async-start(), calls=%async_computation.3 | async-start | bytes 2097152 | tf_op jit(solution)/shard_map/while/body/eval_jaxpr/psum | solution.py:19
  121.2 82.8 %collective-permute-start = (bf16[128,4096]{1,0:T(8,128)(2,1)S(1)}, bf16[128,4096]{1,0:T(8,128)(2,1)}, u32[]{:S(2)}, u32[]{:S(2)}) collective-permute-start(bf16[128,4096]{1,0:T(8,128)(2,1)S(1)} %copy-done), channel_id=1, source_target_pairs={{0,16},{16,32},{32,48},{48,64},{64,80},{80,96},{96,112},{1,17},{17... | collective-permute-start | bytes 3145736 | tf_op jit(solution)/shard_map/while/body/eval_jaxpr/ppermute | solution.py:14
  125.0 79.0 %copy-start.5 = (f32[4096]{0:T(1024)S(1)}, f32[4096]{0:T(1024)}, u32[]{:S(2)}) copy-start(f32[4096]{0:T(1024)} %get-tuple-element.671) | copy-start | bytes 49156 | tf_op jit(solution)/shard_map/while
  125.0 79.0 %copy-start.8 = (f32[1,4]{1,0:T(1,128)S(1)}, f32[1,4]{1,0:T(1,128)}, u32[]{:S(2)}) copy-start(f32[1,4]{1,0:T(1,128)} %get-tuple-element.697) | copy-start | bytes 52 | tf_op jit(solution)/shard_map/while
  204.0 74.7 %reduce-scatter.2.cloned.1.call-start = ((), (), s32[]{:S(2)}) async-start(), calls=%async_computation.1 | async-start | bytes 1114112 | tf_op jit(solution)/shard_map/while/body/eval_jaxpr/reduce_scatter | solution.py:90
  204.7 2.9 copy-start.6
  219.0 100.9 %all-gather.2.cloned.1.call-start = ((), (), s32[]{:S(2)}) async-start(), calls=%async_computation.2 | async-start | bytes 1114112 | tf_op jit(solution)/shard_map/while/body/eval_jaxpr/all_gather | solution.py:123
  280.3 123.6 %all-reduce.2.cloned.1.call-start = ((), (), s32[]{:S(2)}) async-start(), calls=%async_computation.3 | async-start | bytes 2097152 | tf_op jit(solution)/shard_map/while/body/eval_jaxpr/psum | solution.py:19
  321.5 82.6 %collective-permute-start = (bf16[128,4096]{1,0:T(8,128)(2,1)S(1)}, bf16[128,4096]{1,0:T(8,128)(2,1)}, u32[]{:S(2)}, u32[]{:S(2)}) collective-permute-start(bf16[128,4096]{1,0:T(8,128)(2,1)S(1)} %copy-done), channel_id=1, source_target_pairs={{0,16},{16,32},{32,48},{48,64},{64,80},{80,96},{96,112},{1,17},{17... | collective-permute-start | bytes 3145736 | tf_op jit(solution)/shard_map/while/body/eval_jaxpr/ppermute | solution.py:14
  325.3 78.9 %copy-start.5 = (f32[4096]{0:T(1024)S(1)}, f32[4096]{0:T(1024)}, u32[]{:S(2)}) copy-start(f32[4096]{0:T(1024)} %get-tuple-element.671) | copy-start | bytes 49156 | tf_op jit(solution)/shard_map/while
  325.3 78.9 %copy-start.8 = (f32[1,4]{1,0:T(1,128)S(1)}, f32[1,4]{1,0:T(1,128)}, u32[]{:S(2)}) copy-start(f32[1,4]{1,0:T(1,128)} %get-tuple-element.697) | copy-start | bytes 52 | tf_op jit(solution)/shard_map/while
  404.2 74.7 %reduce-scatter.2.cloned.1.call-start = ((), (), s32[]{:S(2)}) async-start(), calls=%async_computation.1 | async-start | bytes 1114112 | tf_op jit(solution)/shard_map/while/body/eval_jaxpr/reduce_scatter | solution.py:90
  404.8 2.9 copy-start.6
  419.2 101.1 %all-gather.2.cloned.1.call-start = ((), (), s32[]{:S(2)}) async-start(), calls=%async_computation.2 | async-start | bytes 1114112 | tf_op jit(solution)/shard_map/while/body/eval_jaxpr/all_gather | solution.py:123
  480.4 123.8 %all-reduce.2.cloned.1.call-start = ((), (), s32[]{:S(2)}) async-start(), calls=%async_computation.3 | async-start | bytes 2097152 | tf_op jit(solution)/shard_map/while/body/eval_jaxpr/psum | solution.py:19
  521.9 83.9 %collective-permute-start = (bf16[128,4096]{1,0:T(8,128)(2,1)S(1)}, bf16[128,4096]{1,0:T(8,128)(2,1)}, u32[]{:S(2)}, u32[]{:S(2)}) collective-permute-start(bf16[128,4096]{1,0:T(8,128)(2,1)S(1)} %copy-done), channel_id=1, source_target_pairs={{0,16},{16,32},{32,48},{48,64},{64,80},{80,96},{96,112},{1,17},{17... | collective-permute-start | bytes 3145736 | tf_op jit(solution)/shard_map/while/body/eval_jaxpr/ppermute | solution.py:14
  525.6 80.2 %copy-start.5 = (f32[4096]{0:T(1024)S(1)}, f32[4096]{0:T(1024)}, u32[]{:S(2)}) copy-start(f32[4096]{0:T(1024)} %get-tuple-element.671) | copy-start | bytes 49156 | tf_op jit(solution)/shard_map/while
  525.6 80.2 %copy-start.8 = (f32[1,4]{1,0:T(1,128)S(1)}, f32[1,4]{1,0:T(1,128)}, u32[]{:S(2)}) copy-start(f32[1,4]{1,0:T(1,128)} %get-tuple-element.697) | copy-start | bytes 52 | tf_op jit(solution)/shard_map/while
  605.8 74.3 %reduce-scatter.2.cloned.1.call-start = ((), (), s32[]{:S(2)}) async-start(), calls=%async_computation.1 | async-start | bytes 1114112 | tf_op jit(solution)/shard_map/while/body/eval_jaxpr/reduce_scatter | solution.py:90
  606.5 2.9 copy-start.6
  620.8 101.1 %all-gather.2.cloned.1.call-start = ((), (), s32[]{:S(2)}) async-start(), calls=%async_computation.2 | async-start | bytes 1114112 | tf_op jit(solution)/shard_map/while/body/eval_jaxpr/all_gather | solution.py:123
  681.6 124.2 %all-reduce.2.cloned.1.call-start = ((), (), s32[]{:S(2)}) async-start(), calls=%async_computation.3 | async-start | bytes 2097152 | tf_op jit(solution)/shard_map/while/body/eval_jaxpr/psum | solution.py:19
  723.6 83.9 %collective-permute-start = (bf16[128,4096]{1,0:T(8,128)(2,1)S(1)}, bf16[128,4096]{1,0:T(8,128)(2,1)}, u32[]{:S(2)}, u32[]{:S(2)}) collective-permute-start(bf16[128,4096]{1,0:T(8,128)(2,1)S(1)} %copy-done), channel_id=1, source_target_pairs={{0,16},{16,32},{32,48},{48,64},{64,80},{80,96},{96,112},{1,17},{17... | collective-permute-start | bytes 3145736 | tf_op jit(solution)/shard_map/while/body/eval_jaxpr/ppermute | solution.py:14
  727.3 80.1 %copy-start.5 = (f32[4096]{0:T(1024)S(1)}, f32[4096]{0:T(1024)}, u32[]{:S(2)}) copy-start(f32[4096]{0:T(1024)} %get-tuple-element.671) | copy-start | bytes 49156 | tf_op jit(solution)/shard_map/while
  727.3 80.1 %copy-start.8 = (f32[1,4]{1,0:T(1,128)S(1)}, f32[1,4]{1,0:T(1,128)}, u32[]{:S(2)}) copy-start(f32[1,4]{1,0:T(1,128)} %get-tuple-element.697) | copy-start | bytes 52 | tf_op jit(solution)/shard_map/while
  807.5 74.3 %reduce-scatter.2.cloned.1.call-start = ((), (), s32[]{:S(2)}) async-start(), calls=%async_computation.1 | async-start | bytes 1114112 | tf_op jit(solution)/shard_map/while/body/eval_jaxpr/reduce_scatter | solution.py:90
  808.1 2.9 copy-start.6
  822.5 100.8 %all-gather.2.cloned.1.call-start = ((), (), s32[]{:S(2)}) async-start(), calls=%async_computation.2 | async-start | bytes 1114112 | tf_op jit(solution)/shard_map/while/body/eval_jaxpr/all_gather | solution.py:123
  883.3 123.9 %all-reduce.2.cloned.1.call-start = ((), (), s32[]{:S(2)}) async-start(), calls=%async_computation.3 | async-start | bytes 2097152 | tf_op jit(solution)/shard_map/while/body/eval_jaxpr/psum | solution.py:19
  924.9 82.6 %collective-permute-start = (bf16[128,4096]{1,0:T(8,128)(2,1)S(1)}, bf16[128,4096]{1,0:T(8,128)(2,1)}, u32[]{:S(2)}, u32[]{:S(2)}) collective-permute-start(bf16[128,4096]{1,0:T(8,128)(2,1)S(1)} %copy-done), channel_id=1, source_target_pairs={{0,16},{16,32},{32,48},{48,64},{64,80},{80,96},{96,112},{1,17},{17... | collective-permute-start | bytes 3145736 | tf_op jit(solution)/shard_map/while/body/eval_jaxpr/ppermute | solution.py:14
  928.7 78.9 %copy-start.5 = (f32[4096]{0:T(1024)S(1)}, f32[4096]{0:T(1024)}, u32[]{:S(2)}) copy-start(f32[4096]{0:T(1024)} %get-tuple-element.671) | copy-start | bytes 49156 | tf_op jit(solution)/shard_map/while
  928.7 78.9 %copy-start.8 = (f32[1,4]{1,0:T(1,128)S(1)}, f32[1,4]{1,0:T(1,128)}, u32[]{:S(2)}) copy-start(f32[1,4]{1,0:T(1,128)} %get-tuple-element.697) | copy-start | bytes 52 | tf_op jit(solution)/shard_map/while
  1007.6 74.7 %reduce-scatter.2.cloned.1.call-start = ((), (), s32[]{:S(2)}) async-start(), calls=%async_computation.1 | async-start | bytes 1114112 | tf_op jit(solution)/shard_map/while/body/eval_jaxpr/reduce_scatter | solution.py:90
  1008.2 2.9 copy-start.6
  1022.6 101.0 %all-gather.2.cloned.1.call-start = ((), (), s32[]{:S(2)}) async-start(), calls=%async_computation.2 | async-start | bytes 1114112 | tf_op jit(solution)/shard_map/while/body/eval_jaxpr/all_gather | solution.py:123
  1083.8 123.7 %all-reduce.2.cloned.1.call-start = ((), (), s32[]{:S(2)}) async-start(), calls=%async_computation.3 | async-start | bytes 2097152 | tf_op jit(solution)/shard_map/while/body/eval_jaxpr/psum | solution.py:19
  1125.2 82.6 %collective-permute-start = (bf16[128,4096]{1,0:T(8,128)(2,1)S(1)}, bf16[128,4096]{1,0:T(8,128)(2,1)}, u32[]{:S(2)}, u32[]{:S(2)}) collective-permute-start(bf16[128,4096]{1,0:T(8,128)(2,1)S(1)} %copy-done), channel_id=1, source_target_pairs={{0,16},{16,32},{32,48},{48,64},{64,80},{80,96},{96,112},{1,17},{17... | collective-permute-start | bytes 3145736 | tf_op jit(solution)/shard_map/while/body/eval_jaxpr/ppermute | solution.py:14
  1128.9 78.9 %copy-start.5 = (f32[4096]{0:T(1024)S(1)}, f32[4096]{0:T(1024)}, u32[]{:S(2)}) copy-start(f32[4096]{0:T(1024)} %get-tuple-element.671) | copy-start | bytes 49156 | tf_op jit(solution)/shard_map/while
  1128.9 78.9 %copy-start.8 = (f32[1,4]{1,0:T(1,128)S(1)}, f32[1,4]{1,0:T(1,128)}, u32[]{:S(2)}) copy-start(f32[1,4]{1,0:T(1,128)} %get-tuple-element.697) | copy-start | bytes 52 | tf_op jit(solution)/shard_map/while
  1207.9 74.7 %reduce-scatter.2.cloned.1.call-start = ((), (), s32[]{:S(2)}) async-start(), calls=%async_computation.1 | async-start | bytes 1114112 | tf_op jit(solution)/shard_map/while/body/eval_jaxpr/reduce_scatter | solution.py:90
  1208.5 2.9 copy-start.6
  1222.9 101.0 %all-gather.2.cloned.1.call-start = ((), (), s32[]{:S(2)}) async-start(), calls=%async_computation.2 | async-start | bytes 1114112 | tf_op jit(solution)/shard_map/while/body/eval_jaxpr/all_gather | solution.py:123
  1284.1 123.7 %all-reduce.2.cloned.1.call-start = ((), (), s32[]{:S(2)}) async-start(), calls=%async_computation.3 | async-start | bytes 2097152 | tf_op jit(solution)/shard_map/while/body/eval_jaxpr/psum | solution.py:19
  1325.5 82.7 %collective-permute-start = (bf16[128,4096]{1,0:T(8,128)(2,1)S(1)}, bf16[128,4096]{1,0:T(8,128)(2,1)}, u32[]{:S(2)}, u32[]{:S(2)}) collective-permute-start(bf16[128,4096]{1,0:T(8,128)(2,1)S(1)} %copy-done), channel_id=1, source_target_pairs={{0,16},{16,32},{32,48},{48,64},{64,80},{80,96},{96,112},{1,17},{17... | collective-permute-start | bytes 3145736 | tf_op jit(solution)/shard_map/while/body/eval_jaxpr/ppermute | solution.py:14
  1329.2 79.0 %copy-start.5 = (f32[4096]{0:T(1024)S(1)}, f32[4096]{0:T(1024)}, u32[]{:S(2)}) copy-start(f32[4096]{0:T(1024)} %get-tuple-element.671) | copy-start | bytes 49156 | tf_op jit(solution)/shard_map/while
  1329.2 79.0 %copy-start.8 = (f32[1,4]{1,0:T(1,128)S(1)}, f32[1,4]{1,0:T(1,128)}, u32[]{:S(2)}) copy-start(f32[1,4]{1,0:T(1,128)} %get-tuple-element.697) | copy-start | bytes 52 | tf_op jit(solution)/shard_map/while
  1408.2 74.8 %reduce-scatter.2.cloned.1.call-start = ((), (), s32[]{:S(2)}) async-start(), calls=%async_computation.1 | async-start | bytes 1114112 | tf_op jit(solution)/shard_map/while/body/eval_jaxpr/reduce_scatter | solution.py:90
  1408.8 2.9 copy-start.6
  1423.2 101.1 %all-gather.2.cloned.1.call-start = ((), (), s32[]{:S(2)}) async-start(), calls=%async_computation.2 | async-start | bytes 1114112 | tf_op jit(solution)/shard_map/while/body/eval_jaxpr/all_gather | solution.py:123
  1484.5 123.7 %all-reduce.2.cloned.1.call-start = ((), (), s32[]{:S(2)}) async-start(), calls=%async_computation.3 | async-start | bytes 2097152 | tf_op jit(solution)/shard_map/while/body/eval_jaxpr/psum | solution.py:19
  1525.9 82.6 %collective-permute-start = (bf16[128,4096]{1,0:T(8,128)(2,1)S(1)}, bf16[128,4096]{1,0:T(8,128)(2,1)}, u32[]{:S(2)}, u32[]{:S(2)}) collective-permute-start(bf16[128,4096]{1,0:T(8,128)(2,1)S(1)} %copy-done), channel_id=1, source_target_pairs={{0,16},{16,32},{32,48},{48,64},{64,80},{80,96},{96,112},{1,17},{17... | collective-permute-start | bytes 3145736 | tf_op jit(solution)/shard_map/while/body/eval_jaxpr/ppermute | solution.py:14
  1529.6 78.9 %copy-start.5 = (f32[4096]{0:T(1024)S(1)}, f32[4096]{0:T(1024)}, u32[]{:S(2)}) copy-start(f32[4096]{0:T(1024)} %get-tuple-element.671) | copy-start | bytes 49156 | tf_op jit(solution)/shard_map/while
  1529.6 78.9 %copy-start.8 = (f32[1,4]{1,0:T(1,128)S(1)}, f32[1,4]{1,0:T(1,128)}, u32[]{:S(2)}) copy-start(f32[1,4]{1,0:T(1,128)} %get-tuple-element.697) | copy-start | bytes 52 | tf_op jit(solution)/shard_map/while
  1608.6 74.9 %reduce-scatter.2.cloned.1.call-start = ((), (), s32[]{:S(2)}) async-start(), calls=%async_computation.1 | async-start | bytes 1114112 | tf_op jit(solution)/shard_map/while/body/eval_jaxpr/reduce_scatter | solution.py:90
  1609.2 2.9 copy-start.6
  1623.6 100.9 %all-gather.2.cloned.1.call-start = ((), (), s32[]{:S(2)}) async-start(), calls=%async_computation.2 | async-start | bytes 1114112 | tf_op jit(solution)/shard_map/while/body/eval_jaxpr/all_gather | solution.py:123
  1685.0 123.4 %all-reduce.2.cloned.1.call-start = ((), (), s32[]{:S(2)}) async-start(), calls=%async_computation.3 | async-start | bytes 2097152 | tf_op jit(solution)/shard_map/while/body/eval_jaxpr/psum | solution.py:19
  1726.1 82.6 %collective-permute-start = (bf16[128,4096]{1,0:T(8,128)(2,1)S(1)}, bf16[128,4096]{1,0:T(8,128)(2,1)}, u32[]{:S(2)}, u32[]{:S(2)}) collective-permute-start(bf16[128,4096]{1,0:T(8,128)(2,1)S(1)} %copy-done), channel_id=1, source_target_pairs={{0,16},{16,32},{32,48},{48,64},{64,80},{80,96},{96,112},{1,17},{17... | collective-permute-start | bytes 3145736 | tf_op jit(solution)/shard_map/while/body/eval_jaxpr/ppermute | solution.py:14
  1729.9 78.9 %copy-start.5 = (f32[4096]{0:T(1024)S(1)}, f32[4096]{0:T(1024)}, u32[]{:S(2)}) copy-start(f32[4096]{0:T(1024)} %get-tuple-element.671) | copy-start | bytes 49156 | tf_op jit(solution)/shard_map/while
  1729.9 78.9 %copy-start.8 = (f32[1,4]{1,0:T(1,128)S(1)}, f32[1,4]{1,0:T(1,128)}, u32[]{:S(2)}) copy-start(f32[1,4]{1,0:T(1,128)} %get-tuple-element.697) | copy-start | bytes 52 | tf_op jit(solution)/shard_map/while
  (29 other events, 47.6 us)
Sparse Core Ops, SparseCore 0:
  24.6 53.8 reduce-scatter.1
  80.2 39.3 all-gather.1
  122.1 81.4 all-reduce.1
  219.2 59.5 reduce-scatter.1
  280.4 39.4 all-gather.1
  322.3 81.5 all-reduce.1
  419.3 59.5 reduce-scatter.1
  480.6 39.5 all-gather.1
  522.8 81.3 all-reduce.1
  621.0 59.1 reduce-scatter.1
  681.9 40.0 all-gather.1
  724.3 81.5 all-reduce.1
  822.6 59.1 reduce-scatter.1
  883.4 39.8 all-gather.1
  925.7 81.4 all-reduce.1
  1022.7 59.5 reduce-scatter.1
  1083.9 39.5 all-gather.1
  1125.9 81.5 all-reduce.1
  1223.0 59.5 reduce-scatter.1
  1284.2 39.5 all-gather.1
  1326.4 81.3 all-reduce.1
  1423.3 59.5 reduce-scatter.1
  1484.7 39.5 all-gather.1
  1526.6 81.5 all-reduce.1
  1623.7 59.6 reduce-scatter.1
  1685.1 39.3 all-gather.1
  1726.9 81.4 all-reduce.1
where the time goes:
time: 1830 us; the launch traced here: 1820 us
  waiting for transfers between devices  1600 us (87%)
  other arithmetic  91.7 us (5%)
  matrix products  74.6 us (4%)
  local copies, waits for them, and re-layouts  25.1 us (1%)
    psum x9, waiting for transfers between devices, broadcast(): return lax.psum(kept, axis)  707 us
    reduce_scatter x9, waiting for transfers between devices, layer(): lax.psum_scatter(jnp.dot(blended_payloads, w_output, preferred_element_ty...  531 us
    all_gather x9, waiting for transfers between devices, advance(): outgoing = lax.all_gather(share, 'seq', axis=0, tiled=True)  358 us
  transfers between devices with their start and end apart: 36, of which 27 were waited for; matrix products, arithmetic and copies ran while one was open for 2% of the time, Pallas kernels for 0%

commit v1 on v0

v1 whole, which is shorter than its diff:
```python
import functools

import jax
import jax.numpy as jnp
from jax import lax
from jax.experimental import pallas as pl
from jax.experimental.pallas import tpu as pltpu
from jax.sharding import PartitionSpec as P

MESH = pl.DeviceIdType.MESH
EPS = 1e-06
F32 = jnp.float32
BF16 = jnp.bfloat16

RING = 4


def kernel(
    inbound,
    decoder,
    w_query,
    w_key,
    w_value,
    w_out,
    gain,
    sharpness,
    last_gain,
    result,
    weights,
    out_weights,
    x_buf,
    mix_buf,
    mem_buf,
    out_buf,
    q_unit,
    k_unit,
    v_rows,
    acc,
    squares,
    out_acc,
    x_recv,
    mix_recv,
    mem_recv,
    out_recv,
    x_send,
    mix_send,
    mem_send,
    out_send,
    next_send,
    wo_recv,
    wo_send,
    load_sem,
    x_load,
    store_sem,
):
    sections = lax.axis_size("section")
    seq = lax.axis_size("seq")
    encoders = 3 * sections // 8
    section = lax.axis_index("section")
    me = lax.axis_index("seq")
    batches, blocks, length, width = x_buf.shape
    features = blocks * width
    half = length // 2
    heads = sharpness.shape[1]
    head_size = width // heads
    x_pos, y_pos, core = me // 4, (me // 2) % 2, me % 2

    def at(dx, dy, dc):
        return ((x_pos + dx) % RING) * 4 + ((y_pos + dy) % 2) * 2 + (core + dc) % 2

    def columns(j):
        return pl.ds(pl.multiple_of(j * width, width), width)

    loads = [
        pltpu.make_async_copy(
            w_ref.at[0], weights.at[:, pl.ds(i * width, width)], load_sem.at[i]
        )
        for i, w_ref in enumerate((w_query, w_key, w_value))
    ]
    for load in loads:
        load.start()

    def load_x(source):
        for m in range(batches):

            def one(j, carry):
                pltpu.make_async_copy(
                    source.at[m, :, columns(j)], x_buf.at[m, j], x_load.at[m]
                ).start()
                return carry

            lax.fori_loop(0, blocks, one, 0)

    pl.when(section == 0)(lambda: load_x(inbound))
    pl.when(section == encoders)(lambda: load_x(decoder))
    own_wo = pltpu.make_async_copy(w_out.at[0, :, columns(me)], out_weights.at[me], load_sem.at[3])
    own_wo.start()

    barrier = pltpu.get_barrier_semaphore()

    def greet_peer(i, carry):
        pl.semaphore_signal(
            barrier, inc=1, device_id=(section, (me + i) % seq), device_id_type=MESH
        )
        return carry

    def greet_section(i, carry):
        pl.semaphore_signal(
            barrier, inc=1, device_id=((section + i) % sections, me), device_id_type=MESH
        )
        return carry

    lax.fori_loop(1, seq, greet_peer, 0)
    lax.fori_loop(1, sections, greet_section, 0)
    pl.semaphore_wait(barrier, seq - 1 + sections - 1)

    def wo_copy(i):
        peer = (me + i) % seq
        return pltpu.make_async_remote_copy(
            src_ref=w_out.at[0, :, columns(peer)],
            dst_ref=out_weights.at[me],
            send_sem=wo_send.at[i],
            recv_sem=wo_recv.at[me],
            device_id=(section, peer),
            device_id_type=MESH,
        )

    def wo_start(i, carry):
        wo_copy(i).start()
        return carry

    lax.fori_loop(1, seq, wo_start, 0)

    def wo_wait(i, carry):
        peer = (me + i) % seq
        pltpu.make_async_remote_copy(
            src_ref=out_weights.at[peer],
            dst_ref=out_weights.at[peer],
            send_sem=wo_send.at[i],
            recv_sem=wo_recv.at[peer],
            device_id=(section, peer),
            device_id_type=MESH,
        ).wait_recv()
        return carry

    own_targets = ((1, 0, 0), (-1, 0, 0), (1, 1, 0), (-1, 1, 0), (0, 1, 0), (0, 0, 1))
    relayed = (
        ((1, 0, 0), 0, (-1, 0, 0)),
        ((-1, 0, 0), 1, (1, 0, 0)),
        ((1, 1, 0), 0, (-1, 0, 0)),
        ((-1, 1, 0), 1, (1, 0, 0)),
    )
    handed = ((1, 0, 0), (-1, 0, 0), (0, 1, 0), (1, 1, 0), (-1, 1, 0), (2, 0, 0), (2, 1, 0))

    class Gather:
        def __init__(self, buf, recv, send):
            self.buf, self.recv, self.send = buf, recv, send

        def copy(self, m, index):
            if index < 6:
                j, part, target = me, None, own_targets[index]
            elif index < 10:
                where, part, target = relayed[index - 6]
                j = at(*where)
            else:
                j, part, target = at(*handed[index - 10]), None, (0, 0, 1)
            ref = self.buf.at[m, j]
            if part is not None:
                ref = self.buf.at[m, j, pl.ds(part * half, half)]
            return pltpu.make_async_remote_copy(
                src_ref=ref,
                dst_ref=ref,
                send_sem=self.send.at[m, index],
                recv_sem=self.recv.at[m, 2 * j + (part or 0)],
                device_id=(section, at(*target)),
                device_id_type=MESH,
            )

        def begin(self, m):
            for index in range(6):
                self.copy(m, index).start()

        def arrived(self, m, j, part=None):
            ref = self.buf.at[m, j]
            if part is not None:
                ref = self.buf.at[m, j, pl.ds(part * half, half)]
            pltpu.make_async_remote_copy(
                src_ref=ref,
                dst_ref=ref,
                send_sem=self.send.at[m, 0],
                recv_sem=self.recv.at[m, 2 * j + (part or 0)],
                device_id=(section, at(0, 0, 1)),
                device_id_type=MESH,
            ).wait_recv()

        def entered(self, m):
            self.arrived(m, me)

        def process(self, m, use):
            def chip(dx, dy):
                self.arrived(m, at(dx, dy, 1))
                use(m, at(dx, dy, 0) // 2)

            self.arrived(m, at(1, 0, 0))
            self.copy(m, 6).start()
            self.copy(m, 10).start()
            self.arrived(m, at(-1, 0, 0))
            self.copy(m, 7).start()
            self.copy(m, 11).start()
            chip(0, 0)
            self.arrived(m, at(0, 1, 0))
            self.copy(m, 12).start()
            self.arrived(m, at(1, 1, 0))
            self.copy(m, 8).start()
            self.copy(m, 13).start()
            self.arrived(m, at(-1, 1, 0))
            self.copy(m, 9).start()
            self.copy(m, 14).start()
            chip(1, 0)
            chip(-1, 0)
            chip(0, 1)
            self.arrived(m, at(2, 0, 0), 0)
            self.arrived(m, at(2, 0, 0), 1)
            self.copy(m, 15).start()
            chip(1, 1)
            chip(-1, 1)
            self.arrived(m, at(2, 1, 0), 0)
            self.arrived(m, at(2, 1, 0), 1)
            self.copy(m, 16).start()
            chip(2, 0)
            chip(2, 1)

        def drain(self, m):
            for index in range(17):
                self.copy(m, index).wait_send()

    x_gather = Gather(x_buf, x_recv, x_send)
    mix_gather = Gather(mix_buf, mix_recv, mix_send)
    mem_gather = Gather(mem_buf, mem_recv, mem_send)
    out_gather = Gather(out_buf, out_recv, out_send)

    def clear():
        acc[...] = jnp.zeros_like(acc)
        squares[...] = jnp.zeros_like(squares)

    def project_block(buf, gains, first, stop, m, j):
        rows = buf[m, j].astype(F32)
        square = rows * rows
        squares[...] += square[:, : width // 2] + square[:, width // 2 :]
        scaled = (rows * gains[:, columns(j)]).astype(BF16)
        acc[:, first:stop] += jnp.dot(
            scaled, weights[columns(j), first:stop], preferred_element_type=F32
        )

    def projecting(buf, gains, first, stop):
        def use(m, q):
            project_block(buf, gains, first, stop, m, 2 * q)
            project_block(buf, gains, first, stop, m, 2 * q + 1)

        return use

    def local_project(m, gains, first, stop):
        clear()
        pltpu.make_async_copy(x_buf.at[m], x_buf.at[m], x_load.at[m]).wait()

        def one(j, carry):
            project_block(x_buf, gains, first, stop, m, j)
            return carry

        lax.fori_loop(0, blocks, one, 0)

    def gathered_project(gather, m, gains, first, stop):
        clear()
        gather.entered(m)
        gather.begin(m)
        gather.process(m, projecting(gather.buf, gains, first, stop))

    def row_factor():
        return lax.rsqrt(jnp.sum(squares[...], axis=1, keepdims=True) * (1.0 / features) + EPS)

    def unit(projected):
        square = projected * projected
        upper = square.astype(BF16)
        lower = (square - upper.astype(F32)).astype(BF16)
        row = lax.broadcasted_iota(jnp.int32, (width, width), 0) // head_size
        column = lax.broadcasted_iota(jnp.int32, (width, width), 1) // head_size
        spread = jnp.where(row == column, 1.0 / head_size, 0.0).astype(BF16)
        mean = jnp.dot(upper, spread, preferred_element_type=F32) + jnp.dot(
            lower, spread, preferred_element_type=F32
        )
        return (projected * lax.rsqrt(mean + EPS)).astype(BF16)

    def keep_query(m):
        q_unit[m] = unit(acc[:, :width] * row_factor())

    def keep_memory(m):
        factor = row_factor()
        k_unit[m] = unit(acc[:, width : 2 * width] * factor)
        v_rows[m] = (acc[:, 2 * width :] * factor).astype(BF16)

    def attend(m):
        queries = q_unit[m].astype(F32)
        keys = k_unit[m]
        values = v_rows[m]
        lane_head = lax.broadcasted_iota(jnp.int32, (length, width), 1) // head_size
        stacked = jnp.concatenate(
            [jnp.where(lane_head == h, queries, 0.0).astype(BF16) for h in range(heads)], axis=0
        )
        scores = lax.dot_general(
            stacked, keys, (((1,), (1,)), ((), ())), preferred_element_type=F32
        )
        mixture = jnp.zeros((length, width), F32)
        for h in range(heads):
            factor = sharpness[0, h] * (1.0 / head_size**0.5)
            grown = jnp.exp(scores[h * length : (h + 1) * length] * factor)
            total = jnp.sum(grown, axis=1, keepdims=True)
            share = (grown * (1.0 / total)).astype(BF16)
            mixed = jnp.dot(share, values, preferred_element_type=F32)
            mixture = jnp.where(lane_head == h, mixed, mixture)
        mix_buf[m, me] = mixture.astype(BF16)
        mix_gather.begin(m)

    full = 3 * width
    for load in loads:
        load.wait()

    def early(m, carry):
        @pl.when(section == encoders)
        def _():
            local_project(m, gain, 0, width)
            keep_query(m)

        @pl.when(section > encoders)
        def _():
            gathered_project(mem_gather, m, last_gain, width, full)
            keep_memory(m)

        return carry

    lax.fori_loop(0, batches, early, 0)

    def main(m, carry):
        @pl.when(section == 0)
        def _():
            local_project(m, gain, 0, full)

        @pl.when((section > 0) & (section < encoders))
        def _():
            gathered_project(x_gather, m, gain, 0, full)

        @pl.when(section < encoders)
        def _():
            keep_query(m)
            keep_memory(m)

        @pl.when(section == encoders)
        def _():
            gathered_project(mem_gather, m, last_gain, width, full)
            keep_memory(m)

        @pl.when(section > encoders)
        def _():
            gathered_project(x_gather, m, gain, 0, width)
            keep_query(m)

        attend(m)
        return carry

    lax.fori_loop(0, batches, main, 0)

    own_wo.wait()
    lax.fori_loop(1, seq, wo_wait, 0)

    def onward(m, target):
        return pltpu.make_async_remote_copy(
            src_ref=out_buf.at[m, me],
            dst_ref=x_buf.at[m, me],
            send_sem=next_send.at[m, 0],
            recv_sem=x_recv.at[m, 2 * me],
            device_id=(target, me),
            device_id_type=MESH,
        )

    def to_memory(m, i):
        return pltpu.make_async_remote_copy(
            src_ref=out_buf.at[m, me],
            dst_ref=mem_buf.at[m, me],
            send_sem=next_send.at[m, i],
            recv_sem=mem_recv.at[m, 2 * me],
            device_id=(encoders + i, me),
            device_id_type=MESH,
        )

    def project_out(m, q):
        for i in range(2):
            j = 2 * q + i
            out_acc[...] += jnp.dot(mix_buf[m, j], out_weights[j], preferred_element_type=F32)

    def finish(m, carry):
        out_acc[...] = x_buf[m, me].astype(F32)
        mix_gather.process(m, project_out)
        out_buf[m, me] = out_acc[...].astype(BF16)

        @pl.when((section < sections - 1) & (section != encoders - 1))
        def _():
            onward(m, section + 1).start()

        @pl.when(section == encoders - 1)
        def _():
            for i in range(sections - encoders):
                to_memory(m, i).start()

        return carry

    lax.fori_loop(0, batches, finish, 0)

    def store(m, q):
        for i in range(2):
            j = 2 * q + i
            pltpu.make_async_copy(
                out_buf.at[m, j], result.at[0, m, :, columns(j)], store_sem.at[m]
            ).start()

    def spread_begin(m, carry):
        out_gather.begin(m)
        return carry

    def spread(m, carry):
        out_gather.process(m, store)
        return carry

    lax.fori_loop(0, batches, spread_begin, 0)
    lax.fori_loop(0, batches, spread, 0)

    def drain(m, carry):
        mix_gather.drain(m)
        out_gather.drain(m)

        @pl.when((section > 0) & (section != encoders))
        def _():
            x_gather.drain(m)

        @pl.when(section >= encoders)
        def _():
            mem_gather.drain(m)

        @pl.when((section < sections - 1) & (section != encoders - 1))
        def _():
            onward(m, section + 1).wait_send()

        @pl.when(section == encoders - 1)
        def _():
            for i in range(sections - encoders):
                to_memory(m, i).wait_send()

        pltpu.make_async_copy(out_buf.at[m], out_buf.at[m], store_sem.at[m]).wait()
        return carry

    lax.fori_loop(0, batches, drain, 0)

    def wo_drain(i, carry):
        wo_copy(i).wait_send()
        return carry

    lax.fori_loop(1, seq, wo_drain, 0)


def solution(mesh):
    sections, seq = mesh.shape["section"], mesh.shape["seq"]

    def shards(inbound, decoder, w_query, w_key, w_value, w_out, gain, sharpness, last_gain):
        batches, length, features = inbound.shape
        width = features // seq
        blocks = pltpu.VMEM((batches, seq, length, width), BF16)
        small = pltpu.VMEM((batches, length, width), BF16)
        recv = pltpu.SemaphoreType.DMA((batches, 2 * seq))
        send = pltpu.SemaphoreType.DMA((batches, 17))
        anywhere = pl.BlockSpec(memory_space=pl.ANY)
        vmem = pl.BlockSpec(memory_space=pltpu.VMEM)
        return pl.pallas_call(
            kernel,
            out_shape=jax.ShapeDtypeStruct((1, batches, length, features), BF16),
            in_specs=[anywhere] * 6 + [vmem, pl.BlockSpec(memory_space=pltpu.SMEM), vmem],
            out_specs=anywhere,
            scratch_shapes=[
                pltpu.VMEM((features, 3 * width), BF16),
                pltpu.VMEM((seq, width, width), BF16),
                blocks,
                blocks,
                blocks,
                blocks,
                small,
                small,
                small,
                pltpu.VMEM((length, 3 * width), F32),
                pltpu.VMEM((length, width // 2), F32),
                pltpu.VMEM((length, width), F32),
                recv,
                recv,
                recv,
                recv,
                send,
                send,
                send,
                send,
                pltpu.SemaphoreType.DMA((batches, sections)),
                pltpu.SemaphoreType.DMA((seq,)),
                pltpu.SemaphoreType.DMA((seq,)),
                pltpu.SemaphoreType.DMA((4,)),
                pltpu.SemaphoreType.DMA((batches,)),
                pltpu.SemaphoreType.DMA((batches,)),
            ],
            compiler_params=pltpu.CompilerParams(
                collective_id=0, has_side_effects=True, vmem_limit_bytes=60 * 1024 * 1024
            ),
            name="cascade",
        )(
            inbound,
            decoder,
            w_query,
            w_key,
            w_value,
            w_out,
            gain,
            sharpness,
            last_gain.reshape(1, features),
        )

    return jax.shard_map(
        shards,
        mesh=mesh,
        in_specs=(
            P(),
            P(),
            P("section", None, "seq"),
            P("section", None, "seq"),
            P("section", None, "seq"),
            P("section", "seq", None),
            P("section", None),
            P("section", "seq"),
            P(),
        ),
        out_specs=P("section", None, None, None),
        check_vma=False,
    )
```

time: 1830 us -> 343 us (0.19)
  waiting for transfers between devices: 1600 us -> 0 us
  Pallas kernels: 0 us -> 340 us
  other arithmetic: 91.7 us -> 0 us
  matrix products: 74.6 us -> 0 us
  local copies, waits for them, and re-layouts: 25.1 us -> 3.13 us
    psum x9 -> x0, waiting for transfers between devices: 707 us -> none  [broadcast(): return lax.psum(kept, axis)]
    reduce_scatter x9 -> x0, waiting for transfers between devices: 531 us -> none  [layer(): lax.psum_scatter(jnp.dot(blended_payloads, w_output, preferred_element_ty...]
    all_gather x9 -> x0, waiting for transfers between devices: 358 us -> none  [advance(): outgoing = lax.all_gather(share, 'seq', axis=0, tiled=True)]
    pallas_call x0 -> x1, Pallas kernels: none -> 340 us  [shards(): pl.pallas_call(kernel, out_shape=jax.ShapeDtypeStruct((1, batches, length...]
    dot_general x54 -> x0, matrix products: 74.6 us -> none  [the longest x9 27.4 us: layer(): jnp.dot(blended_payloads, w_output, preferred_element_type=jnp.float32)]
    select_n x27 -> x0, other arithmetic: 32.7 us -> none  [the longest x9 22 us: advance(): finished = jnp.where(valid, written, finished)]
    reduce_sum x9 -> x0, other arithmetic: 25.5 us -> none  [normalize(): jnp.mean(values * values, axis=-1, keepdims=True) + epsilon]
  transfers between devices with their start and end apart: 36 -> 0, of which waited for: 27 -> 0; matrix products, arithmetic and copies ran while one was open for 2% -> 0% of each run, Pallas kernels for 0% -> 0%
where the time goes in v1:
time: 343 us
  Pallas kernels  340 us (99%)
    pallas_call x1, Pallas kernels, shards(): pl.pallas_call(kernel, out_shape=jax.ShapeDtypeStruct((1, batches, length...  340 us

profile of v1, /device:TPU:123, one launch (start us, length us, event | category | flops | bytes accessed | tf_op | source)
XLA Modules:
  0.0 342.7 jit_solution(9209510804081249501)
XLA Ops:
  0.0 339.5 %cascade.1 = bf16[1,2,128,4096]{3,2,1,0:T(8,128)(2,1)} custom-call(bf16[2,128,4096]{2,1,0:T(8,128)(2,1)} %inbound.1, bf16[2,128,4096]{2,1,0:T(8,128)(2,1)} %decoder.1, bf16[1,4096,256]{2,1,0:T(8,128)(2,1)} %w_query.1, bf16[1,4096,256]{2,1,0:T(8,128)(2,1)} %w_key.1, bf16[1,4096,256]{2,1,0:T(8,128)(2,1)} %w_value.1, bf16[1,256,4096]{2,1,0:T(8,128)(2,1)} %w_out.1, ...), custom_call_target="tpu_custom_call" | custom-call | tf_op jit(solution)/shard_map/cascade/pallas_call | solution.py:480
  339.5 3.1 copy.11

commit v2 on v0

v2 whole, which is shorter than its diff:
```python
import functools

import jax
import jax.numpy as jnp
from jax import lax
from jax.experimental import pallas as pl
from jax.experimental.pallas import tpu as pltpu
from jax.sharding import PartitionSpec as P

MESH = pl.DeviceIdType.MESH
EPS = 1e-06
F32 = jnp.float32
BF16 = jnp.bfloat16

RING = 4
CHIPS = 2 * RING
OTHERS = ((2, 1), (1, 1), (-1, 1), (2, 0), (0, 1), (1, 0), (-1, 0))
PER = 1

QUERY, KEY, VALUE = 0, 1, 2
PLANE = {QUERY: 0, KEY: 2, VALUE: 3}
SQUARES = 1


def kernel(
    inbound,
    decoder,
    w_query,
    w_key,
    w_value,
    w_out,
    gain,
    sharpness,
    last_gain,
    result,
    weights,
    out_weights,
    x_buf,
    mem_buf,
    mix_buf,
    part_buf,
    sum_buf,
    out_buf,
    swap_out,
    swap_in,
    own_acc,
    q_unit,
    k_unit,
    v_rows,
    x_recv,
    mem_recv,
    sum_recv,
    out_recv,
    x_send,
    mem_send,
    sum_send,
    out_send,
    next_send,
    swap_recv,
    swap_send,
    mix_recv,
    mix_send,
    load_sem,
    x_load,
    store_sem,
):
    sections = lax.axis_size("section")
    seq = lax.axis_size("seq")
    encoders = 3 * sections // 8
    section = lax.axis_index("section")
    me = lax.axis_index("seq")
    chunks, _, rows, width = x_buf.shape
    features = seq * width
    length = rows * PER
    heads = sharpness.shape[1]
    head_size = width // heads
    x_pos, y_pos, core = me // 4, (me // 2) % 2, me % 2
    here = me // 2
    partner = 2 * here + 1 - core

    def chip(dx, dy):
        return ((x_pos + dx) % RING) * 2 + (y_pos + dy) % 2

    def columns(j):
        return pl.ds(pl.multiple_of(j * width, width), width)

    def token_rows(ch):
        return pl.ds(pl.multiple_of((ch % PER) * rows, rows), rows)

    def remote(src, dst, send_sem, recv_sem, target):
        return pltpu.make_async_remote_copy(
            src_ref=src,
            dst_ref=dst,
            send_sem=send_sem,
            recv_sem=recv_sem,
            device_id=(section, target),
            device_id_type=MESH,
        )

    def landed(ref, recv_sem):
        remote(ref, ref, mix_send.at[0], recv_sem, partner).wait_recv()

    def load_x(source):
        def one(i, carry):
            ch, q = i // CHIPS, i % CHIPS
            pltpu.make_async_copy(
                source.at[ch // PER, token_rows(ch), columns(2 * q + core)],
                x_buf.at[ch, q],
                x_load.at[0],
            ).start()
            return carry

        lax.fori_loop(0, chunks * CHIPS, one, 0)

    pl.when(section == 0)(lambda: load_x(inbound))
    pl.when(section == encoders)(lambda: load_x(decoder))
    projections = (w_query, w_key, w_value)

    def load_own(q, carry):
        for i, w_ref in enumerate(projections):
            pltpu.make_async_copy(
                w_ref.at[0, columns(2 * q + core)], weights.at[i, q], load_sem.at[0]
            ).start()
        return carry

    def load_own_out(q, carry):
        pltpu.make_async_copy(
            w_out.at[0, :, columns(2 * q + core)], out_weights.at[core, q], load_sem.at[1]
        ).start()
        return carry

    lax.fori_loop(0, CHIPS, load_own, 0)
    lax.fori_loop(0, CHIPS, load_own_out, 0)

    barrier = pltpu.get_barrier_semaphore()

    def greet(target_section, target):
        pl.semaphore_signal(
            barrier, inc=1, device_id=(target_section, target), device_id_type=MESH
        )

    greet(section, partner)
    for other in OTHERS:
        greet(section, 2 * chip(*other) + core)
    lax.fori_loop(1, sections, lambda i, c: (greet((section + i) % sections, me), c)[1], 0)
    pl.semaphore_wait(barrier, CHIPS + sections - 1)

    def give(q, carry):
        for i, w_ref in enumerate(projections):
            remote(
                w_ref.at[0, columns(2 * q + 1 - core)],
                weights.at[3 + i, q],
                load_sem.at[2],
                load_sem.at[3],
                partner,
            ).start()
        return carry

    def give_out(q, carry):
        remote(
            w_out.at[0, :, columns(2 * q + 1 - core)],
            out_weights.at[core, q],
            load_sem.at[4],
            load_sem.at[5],
            partner,
        ).start()
        return carry

    lax.fori_loop(0, CHIPS, give, 0)
    lax.fori_loop(0, CHIPS, give_out, 0)

    def spread(buf, recv, send, ch):
        return [
            remote(
                buf.at[ch, here],
                buf.at[ch, here],
                send.at[ch, i],
                recv.at[ch, here],
                2 * chip(*other) + core,
            )
            for i, other in enumerate(OTHERS)
        ]

    def enter(buf, recv, send, ch):
        landed(buf.at[ch, here], recv.at[ch, here])
        for copy in spread(buf, recv, send, ch):
            copy.start()

    def swap(kind, ch, first, stop):
        return remote(
            swap_out.at[kind, ch, pl.ds(first, stop - first)],
            swap_in.at[kind, ch, pl.ds(first, stop - first)],
            swap_send.at[kind, ch],
            swap_recv.at[kind, ch],
            partner,
        )

    def project(buf, recv, ch, gains, wanted, kind, gathered):
        order = ((0, 0),) + OTHERS
        for first in range(0, CHIPS, 2):
            parts = []
            for other in order[first : first + 2]:
                q = chip(*other)
                if other != (0, 0):
                    pl.when(gathered)(lambda: landed(buf.at[ch, q], recv.at[ch, q]))
                block = buf[ch, q].astype(F32)
                scaled = (block * gains[:, columns(2 * q + core)]).astype(BF16)
                parts.append((q, block * block, scaled))
            square = parts[0][1] + parts[1][1]
            swap_out[kind, ch, SQUARES] = (
                square if first == 0 else swap_out[kind, ch, SQUARES] + square
            )
            for p in wanted:
                for side in range(2):
                    product = sum(
                        jnp.dot(scaled, weights[3 * side + p, q], preferred_element_type=F32)
                        for q, _, scaled in parts
                    )
                    if side == 0:
                        own_acc[p] = product if first == 0 else own_acc[p] + product
                    else:
                        at = PLANE[p]
                        swap_out[kind, ch, at] = (
                            product if first == 0 else swap_out[kind, ch, at] + product
                        )
        first = min(SQUARES, min(PLANE[p] for p in wanted))
        stop = 1 + max(SQUARES, max(PLANE[p] for p in wanted))
        exchange = swap(kind, ch, first, stop)
        exchange.start()
        exchange.wait_recv()
        squares = swap_out[kind, ch, SQUARES] + swap_in[kind, ch, SQUARES]
        factor = lax.rsqrt(jnp.sum(squares, axis=1, keepdims=True) * (1.0 / features) + EPS)
        for p in wanted:
            total = (own_acc[p] + swap_in[kind, ch, PLANE[p]]) * factor
            if p == QUERY:
                q_unit[ch] = unit(total)
            elif p == KEY:
                k_unit[ch // PER, token_rows(ch)] = unit(total)
            else:
                v_rows[ch // PER, token_rows(ch)] = total.astype(BF16)

    def unit(projected):
        square = projected * projected
        upper = square.astype(BF16)
        lower = (square - upper.astype(F32)).astype(BF16)
        row = lax.broadcasted_iota(jnp.int32, (width, width), 0) // head_size
        column = lax.broadcasted_iota(jnp.int32, (width, width), 1) // head_size
        same = jnp.where(row == column, 1.0 / head_size, 0.0).astype(BF16)
        mean = jnp.dot(upper, same, preferred_element_type=F32) + jnp.dot(
            lower, same, preferred_element_type=F32
        )
        return (projected * lax.rsqrt(mean + EPS)).astype(BF16)

    def mix_swap(ch):
        return remote(
            mix_buf.at[ch, core], mix_buf.at[ch, core], mix_send.at[ch], mix_recv.at[ch], partner
        )

    def partial(ch, i):
        q = chip(*OTHERS[i])
        return remote(
            part_buf.at[ch, q],
            sum_buf.at[ch, here],
            sum_send.at[ch, i],
            sum_recv.at[ch, here],
            2 * q + core,
        )

    def attend(ch):
        queries = q_unit[ch].astype(F32)
        keys = k_unit[ch // PER]
        values = v_rows[ch // PER]
        lane_head = lax.broadcasted_iota(jnp.int32, (rows, width), 1) // head_size
        stacked = jnp.concatenate(
            [jnp.where(lane_head == h, queries, 0.0).astype(BF16) for h in range(heads)], axis=0
        )
        scores = lax.dot_general(
            stacked, keys, (((1,), (1,)), ((), ())), preferred_element_type=F32
        )
        mixture = jnp.zeros((rows, width), F32)
        for h in range(heads):
            factor = sharpness[0, h] * (1.0 / head_size**0.5)
            grown = jnp.exp(scores[h * rows : (h + 1) * rows] * factor)
            total = jnp.sum(grown, axis=1, keepdims=True)
            share = (grown * (1.0 / total)).astype(BF16)
            mixed = jnp.dot(share, values, preferred_element_type=F32)
            mixture = jnp.where(lane_head == h, mixed, mixture)
        mix_buf[ch, core] = mixture.astype(BF16)
        mix_swap(ch).start()

    def project_out(ch):
        landed(mix_buf.at[ch, 1 - core], mix_recv.at[ch])
        mixture = [mix_buf[ch, 0], mix_buf[ch, 1]]

        def product(q):
            return sum(
                jnp.dot(mixture[i], out_weights[i, q], preferred_element_type=F32)
                for i in range(2)
            )

        for i, other in enumerate(OTHERS):
            q = chip(*other)
            part_buf[ch, q] = product(q).astype(BF16)
            partial(ch, i).start()
        part_buf[ch, here] = product(here).astype(BF16)

    def onward(ch):
        return pltpu.make_async_remote_copy(
            src_ref=out_buf.at[ch, me],
            dst_ref=x_buf.at[ch, here],
            send_sem=next_send.at[ch, 0],
            recv_sem=x_recv.at[ch, here],
            device_id=(section + 1, me),
            device_id_type=MESH,
        )

    def to_memory(ch, i):
        return pltpu.make_async_remote_copy(
            src_ref=out_buf.at[ch, me],
            dst_ref=mem_buf.at[ch, here],
            send_sem=next_send.at[ch, i],
            recv_sem=mem_recv.at[ch, here],
            device_id=(encoders + i, me),
            device_id_type=MESH,
        )

    def share(ch, i):
        target = 2 * chip(*OTHERS[i]) + core if i < CHIPS - 1 else partner
        return remote(
            out_buf.at[ch, me], out_buf.at[ch, me], out_send.at[ch, i], out_recv.at[ch, me], target
        )

    def hand(ch, i):
        j = 2 * chip(*OTHERS[i]) + core
        return remote(
            out_buf.at[ch, j],
            out_buf.at[ch, j],
            out_send.at[ch, CHIPS + i],
            out_recv.at[ch, j],
            partner,
        )

    def share_begin(ch, carry=0):
        share(ch, CHIPS - 1).start()
        for i in range(CHIPS - 1):
            share(ch, i).start()
        return carry

    def store(ch, j):
        pltpu.make_async_copy(
            out_buf.at[ch, j],
            result.at[0, ch // PER, token_rows(ch), columns(j)],
            store_sem.at[0],
        ).start()

    def share_end(ch, carry):
        store(ch, me)
        for i, other in enumerate(OTHERS):
            j = 2 * chip(*other) + core
            landed(out_buf.at[ch, j], out_recv.at[ch, j])
            hand(ch, i).start()
            store(ch, j)
        for other in ((0, 0),) + OTHERS:
            j = 2 * chip(*other) + 1 - core
            landed(out_buf.at[ch, j], out_recv.at[ch, j])
            store(ch, j)
        return carry

    def reduce(ch):
        total = x_buf[ch, here].astype(F32) + part_buf[ch, here].astype(F32)
        for other in OTHERS:
            q = chip(*other)
            landed(sum_buf.at[ch, q], sum_recv.at[ch, q])
            total = total + sum_buf[ch, q].astype(F32)
        out_buf[ch, me] = total.astype(BF16)

        @pl.when((section < sections - 1) & (section != encoders - 1))
        def _():
            onward(ch).start()

        @pl.when(section == encoders - 1)
        def _():
            for i in range(sections - encoders):
                to_memory(ch, i).start()

        @pl.when(section == sections - 1)
        def _():
            share_begin(ch)

    pltpu.make_async_copy(weights.at[:3], weights.at[:3], load_sem.at[0]).wait()
    remote(weights.at[3:], weights.at[3:], load_sem.at[2], load_sem.at[3], partner).wait()

    @pl.when((section == 0) | (section == encoders))
    def _():
        pltpu.make_async_copy(x_buf, x_buf, x_load.at[0]).wait()

    ahead_x = (x_buf, x_recv)
    ahead_mem = (mem_buf, mem_recv)

    def early_enter(ch, carry):
        enter(mem_buf, mem_recv, mem_send, ch)
        return carry

    def early(ch, carry):
        @pl.when(section == encoders)
        def _():
            project(*ahead_x, ch, gain, (QUERY,), 0, False)

        @pl.when(section > encoders)
        def _():
            project(*ahead_mem, ch, last_gain, (KEY, VALUE), 1, True)

        return carry

    @pl.when(section > encoders)
    def _():
        lax.fori_loop(0, chunks, early_enter, 0)

    @pl.when(section >= encoders)
    def _():
        lax.fori_loop(0, chunks, early, 0)

    pltpu.make_async_copy(out_weights.at[0], out_weights.at[0], load_sem.at[1]).wait()
    remote(out_weights.at[0], out_weights.at[0], load_sem.at[4], load_sem.at[5], partner).wait()

    def begin(ch):
        @pl.when((section > 0) & (section != encoders))
        def _():
            enter(x_buf, x_recv, x_send, ch)

        @pl.when(section == encoders)
        def _():
            enter(mem_buf, mem_recv, mem_send, ch)

    def advance(ch):
        @pl.when(section < encoders)
        def _():
            project(*ahead_x, ch, gain, (QUERY, KEY, VALUE), 0, section > 0)

        @pl.when(section == encoders)
        def _():
            project(*ahead_mem, ch, last_gain, (KEY, VALUE), 1, True)

        @pl.when(section > encoders)
        def _():
            project(*ahead_x, ch, gain, (QUERY,), 0, True)

        if PER == 1:
            attend(ch)
            project_out(ch)
        else:

            @pl.when(section > encoders)
            def _():
                attend(ch)
                project_out(ch)

            @pl.when((section <= encoders) & (ch % PER == PER - 1))
            def _():
                for i in range(PER):
                    attend(ch - PER + 1 + i)
                for i in range(PER):
                    project_out(ch - PER + 1 + i)

    begin(0)

    def step(t, carry):
        pl.when(t + 1 < chunks)(lambda: begin(t + 1))
        pl.when(t < chunks)(lambda: advance(t))
        pl.when(t >= LAG)(lambda: reduce(t - LAG))
        return carry

    LAG = PER
    lax.fori_loop(0, chunks + LAG, step, 0)

    @pl.when(section < sections - 1)
    def _():
        lax.fori_loop(0, chunks, share_begin, 0)

    lax.fori_loop(0, chunks, share_end, 0)

    def drain(ch, carry):
        mix_swap(ch).wait_send()
        for i in range(CHIPS - 1):
            partial(ch, i).wait_send()
            share(ch, i).wait_send()
            hand(ch, i).wait_send()
        share(ch, CHIPS - 1).wait_send()

        @pl.when(section < encoders)
        def _():
            swap(0, ch, 0, 4).wait_send()

        @pl.when(section >= encoders)
        def _():
            swap(0, ch, 0, 2).wait_send()
            swap(1, ch, 1, 4).wait_send()
            for copy in spread(mem_buf, mem_recv, mem_send, ch):
                copy.wait_send()

        @pl.when((section > 0) & (section != encoders))
        def _():
            for copy in spread(x_buf, x_recv, x_send, ch):
                copy.wait_send()

        @pl.when((section < sections - 1) & (section != encoders - 1))
        def _():
            onward(ch).wait_send()

        @pl.when(section == encoders - 1)
        def _():
            for i in range(sections - encoders):
                to_memory(ch, i).wait_send()

        return carry

    lax.fori_loop(0, chunks, drain, 0)
    pltpu.make_async_copy(out_buf, out_buf, store_sem.at[0]).wait()


def solution(mesh):
    sections, seq = mesh.shape["section"], mesh.shape["seq"]

    def shards(inbound, decoder, w_query, w_key, w_value, w_out, gain, sharpness, last_gain):
        batches, length, features = inbound.shape
        width = features // seq
        chunks, rows = batches * PER, length // PER
        dma = pltpu.SemaphoreType.DMA
        blocks = pltpu.VMEM((chunks, CHIPS, rows, width), BF16)
        swapped = pltpu.VMEM((2, chunks, 4, rows, width), F32)
        anywhere = pl.BlockSpec(memory_space=pl.ANY)
        vmem = pl.BlockSpec(memory_space=pltpu.VMEM)
        return pl.pallas_call(
            kernel,
            out_shape=jax.ShapeDtypeStruct((1, batches, length, features), BF16),
            in_specs=[anywhere] * 6 + [vmem, pl.BlockSpec(memory_space=pltpu.SMEM), vmem],
            out_specs=anywhere,
            scratch_shapes=[
                pltpu.VMEM((6, CHIPS, width, width), BF16),
                pltpu.VMEM((2, CHIPS, width, width), BF16),
                blocks,
                blocks,
                pltpu.VMEM((chunks, 2, rows, width), BF16),
                blocks,
                blocks,
                pltpu.VMEM((chunks, seq, rows, width), BF16),
                swapped,
                swapped,
                pltpu.VMEM((3, rows, width), F32),
                pltpu.VMEM((chunks, rows, width), BF16),
                pltpu.VMEM((batches, length, width), BF16),
                pltpu.VMEM((batches, length, width), BF16),
                dma((chunks, CHIPS)),
                dma((chunks, CHIPS)),
                dma((chunks, CHIPS)),
                dma((chunks, seq)),
                dma((chunks, CHIPS - 1)),
                dma((chunks, CHIPS - 1)),
                dma((chunks, CHIPS - 1)),
                dma((chunks, seq)),
                dma((chunks, sections)),
                dma((2, chunks)),
                dma((2, chunks)),
                dma((chunks,)),
                dma((chunks,)),
                dma((6,)),
                dma((1,)),
                dma((1,)),
            ],
            compiler_params=pltpu.CompilerParams(
                collective_id=0, has_side_effects=True, vmem_limit_bytes=60 * 1024 * 1024
            ),
            name="cascade",
        )(
            inbound,
            decoder,
            w_query,
            w_key,
            w_value,
            w_out,
            gain,
            sharpness,
            last_gain.reshape(1, features),
        )

    return jax.shard_map(
        shards,
        mesh=mesh,
        in_specs=(
            P(),
            P(),
            P("section", None, "seq"),
            P("section", None, "seq"),
            P("section", None, "seq"),
            P("section", "seq", None),
            P("section", None),
            P("section", "seq"),
            P(),
        ),
        out_specs=P("section", None, None, None),
        check_vma=False,
    )
```

time: 1830 us -> 220 us (0.12)
  waiting for transfers between devices: 1600 us -> 0 us
  Pallas kernels: 0 us -> 216 us
  other arithmetic: 91.7 us -> 0 us
  matrix products: 74.6 us -> 0 us
  local copies, waits for them, and re-layouts: 25.1 us -> 3.13 us
    psum x9 -> x0, waiting for transfers between devices: 707 us -> none  [broadcast(): return lax.psum(kept, axis)]
    reduce_scatter x9 -> x0, waiting for transfers between devices: 531 us -> none  [layer(): lax.psum_scatter(jnp.dot(blended_payloads, w_output, preferred_element_ty...]
    all_gather x9 -> x0, waiting for transfers between devices: 358 us -> none  [advance(): outgoing = lax.all_gather(share, 'seq', axis=0, tiled=True)]
    pallas_call x0 -> x1, Pallas kernels: none -> 216 us  [shards(): pl.pallas_call(kernel, out_shape=jax.ShapeDtypeStruct((1, batches, length...]
    dot_general x54 -> x0, matrix products: 74.6 us -> none  [the longest x9 27.4 us: layer(): jnp.dot(blended_payloads, w_output, preferred_element_type=jnp.float32)]
    select_n x27 -> x0, other arithmetic: 32.7 us -> none  [the longest x9 22 us: advance(): finished = jnp.where(valid, written, finished)]
    reduce_sum x9 -> x0, other arithmetic: 25.5 us -> none  [normalize(): jnp.mean(values * values, axis=-1, keepdims=True) + epsilon]
  transfers between devices with their start and end apart: 36 -> 0, of which waited for: 27 -> 0; matrix products, arithmetic and copies ran while one was open for 2% -> 0% of each run, Pallas kernels for 0% -> 0%
where the time goes in v2:
time: 220 us; the launch traced here: 219 us
  Pallas kernels  216 us (98%)
  local copies, waits for them, and re-layouts  3.13 us (1%)
    pallas_call x1, Pallas kernels, shards(): pl.pallas_call(kernel, out_shape=jax.ShapeDtypeStruct((1, batches, length...  216 us

profile of v2, /device:TPU:123, one launch (start us, length us, event | category | flops | bytes accessed | tf_op | source)
XLA Modules:
  0.0 218.8 jit_solution(17958077556989444906)
XLA Ops:
  0.0 215.6 %cascade.1 = bf16[1,2,128,4096]{3,2,1,0:T(8,128)(2,1)} custom-call(bf16[2,128,4096]{2,1,0:T(8,128)(2,1)} %inbound.1, bf16[2,128,4096]{2,1,0:T(8,128)(2,1)} %decoder.1, bf16[1,4096,256]{2,1,0:T(8,128)(2,1)} %w_query.1, bf16[1,4096,256]{2,1,0:T(8,128)(2,1)} %w_key.1, bf16[1,4096,256]{2,1,0:T(8,128)(2,1)} %w_value.1, bf16[1,256,4096]{2,1,0:T(8,128)(2,1)} %w_out.1, ...), custom_call_target="tpu_custom_call" | custom-call | tf_op jit(solution)/shard_map/cascade/pallas_call | solution.py:533
  215.7 3.1 %copy.11 = bf16[1,2,128,4096]{3,2,1,0:T(8,128)(2,1)} copy(bf16[1,2,128,4096]{3,2,1,0:T(8,128)(2,1)} %cascade.1) | data formatting | bytes 4194304

commit v3 on v0

v3 whole, which is shorter than its diff:
```python
import jax
import jax.numpy as jnp
from jax import lax
from jax.experimental import pallas as pl
from jax.experimental.pallas import tpu as pltpu
from jax.sharding import PartitionSpec as P

MESH = pl.DeviceIdType.MESH
EPS = 1e-06
F32 = jnp.float32
BF16 = jnp.bfloat16

RING = 4
CHIPS = 2 * RING
CORES = 2
OTHERS = ((2, 1), (1, 1), (-1, 1), (2, 0), (0, 1), (1, 0), (-1, 0))
SUB = 8

QUERY, KEY, VALUE = 0, 1, 2


def kernel(
    inbound,
    decoder,
    w_query,
    w_key,
    w_value,
    w_out,
    gain,
    sharpness,
    last_gain,
    result,
    weights,
    out_weights,
    all_x,
    x_buf,
    mem_buf,
    mix_buf,
    mix_out,
    part_buf,
    sum_buf,
    own_out,
    acc,
    squares,
    q_unit,
    k_unit,
    v_rows,
    sharp,
    x_recv,
    mem_recv,
    sum_recv,
    out_recv,
    x_send,
    mem_send,
    sum_send,
    out_send,
    next_send,
    local_sem,
    pair_recv,
    pair_send,
    gate,
):
    sections = lax.axis_size("section")
    encoders = 3 * sections // 8
    section = lax.axis_index("section")
    me = lax.axis_index("seq")
    _, length, wide = x_buf.shape
    width = wide // CORES
    features = CHIPS * wide
    part = length // SUB
    heads = sharpness.shape[1]
    head_size = width // heads
    x_pos, y_pos, core = me // 4, (me // 2) % 2, me % 2
    here = me // 2
    partner = 2 * here + 1 - core

    def chip(dx, dy):
        return ((x_pos + dx) % RING) * 2 + (y_pos + dy) % 2

    def span(q):
        return pl.ds(pl.multiple_of(q * wide, wide), wide)

    def piece(u):
        return pl.ds(u * part, part)

    def cell(m, u, q):
        return result.at[0, m, piece(u), span(q)]

    def remote(src, dst, send_sem, recv_sem, target):
        return pltpu.make_async_remote_copy(
            src_ref=src,
            dst_ref=dst,
            send_sem=send_sem,
            recv_sem=recv_sem,
            device_id=(section, target),
            device_id_type=MESH,
        )

    def landed(ref, recv_sem):
        remote(ref, ref, pair_send.at[0], recv_sem, partner).wait_recv()

    barrier = pltpu.get_barrier_semaphore()

    def greet(target_section, target):
        pl.semaphore_signal(
            barrier, inc=1, device_id=(target_section, target), device_id_type=MESH
        )

    greet(section, partner)
    for other in OTHERS:
        greet(section, 2 * chip(*other) + core)
    lax.fori_loop(1, sections, lambda i, c: (greet((section + i) % sections, me), c)[1], 0)

    @pl.when(section == 0)
    def _():
        def one(i, carry):
            m, q = i // CHIPS, i % CHIPS
            pltpu.make_async_copy(
                inbound.at[m, :, span(q)], all_x.at[m, q], local_sem.at[0]
            ).start()
            return carry

        lax.fori_loop(0, CORES * CHIPS, one, 0)
        pltpu.make_async_copy(
            inbound.at[core, :, span(here)], x_buf.at[here], local_sem.at[1]
        ).start()

    @pl.when(section == encoders)
    def _():
        def one(q, carry):
            pltpu.make_async_copy(
                decoder.at[core, :, span(q)], x_buf.at[q], local_sem.at[1]
            ).start()
            return carry

        lax.fori_loop(0, CHIPS, one, 0)

    projections = (w_query, w_key, w_value)
    own_weights = [
        pltpu.make_async_copy(w.at[0], weights.at[p, core], local_sem.at[2 + p])
        for p, w in enumerate(projections)
    ]
    own_out_weights = pltpu.make_async_copy(w_out.at[0], out_weights.at[core], local_sem.at[5])
    for copy in own_weights:
        copy.start()
    own_out_weights.start()
    row = lax.broadcasted_iota(jnp.int32, sharp.shape[1:], 0)
    filled = jnp.zeros(sharp.shape[1:], F32)
    for h in range(heads):
        filled = jnp.where(row == h, sharpness[0, h] * (1.0 / head_size**0.5), filled)
    sharp[core] = filled

    give = [
        remote(w.at[0], weights.at[p, core], pair_send.at[p], pair_recv.at[p], partner)
        for p, w in enumerate(projections)
    ]
    give_out = remote(
        w_out.at[0], out_weights.at[core], pair_send.at[3], pair_recv.at[3], partner
    )
    give_sharp = remote(sharp.at[core], sharp.at[core], pair_send.at[4], pair_recv.at[4], partner)
    give_mix = remote(mix_out, mix_buf.at[core], pair_send.at[5], pair_recv.at[5], partner)

    def spread(buf, recv, send, u):
        ref = buf.at[here, piece(u)]
        return [
            remote(ref, ref, send.at[u, i], recv.at[u, here], 2 * chip(*other) + core)
            for i, other in enumerate(OTHERS)
        ]

    def arrive(buf, recv, u, q):
        landed(buf.at[q, piece(u)], recv.at[u, q])

    def enter(buf, recv, send, ahead=None):
        for u in range(SUB):
            arrive(buf, recv, u, here)
            if ahead is not None:
                pl.when(section < sections - 1)(lambda: ahead(buf.at[here], u).start())
            for copy in spread(buf, recv, send, u):
                copy.start()

    def fold(block):
        square = block * block
        return square[:, :width] + square[:, width:]

    def project(buf, recv, gains, wanted, gathered):
        for step, other in enumerate(((0, 0),) + OTHERS):
            q = chip(*other)
            if gathered and step > 0:
                for u in range(SUB):
                    arrive(buf, recv, u, q)
            block = buf[q].astype(F32)
            squares[...] = fold(block) if step == 0 else squares[...] + fold(block)
            scaled = (block * gains[:, span(q)]).astype(BF16)
            for p in wanted:
                for side in range(CORES):
                    product = jnp.dot(
                        scaled, weights[p, side, span(q)], preferred_element_type=F32
                    )
                    acc[p, side] = product if step == 0 else acc[p, side] + product
        factor = row_factor()
        for p in wanted:
            for side in range(CORES):
                keep(p, side, acc[p, side] * factor)

    def project_local(m):
        for q in range(CHIPS):
            block = all_x[m, q].astype(F32)
            squares[...] = fold(block) if q == 0 else squares[...] + fold(block)
            scaled = (block * gain[:, span(q)]).astype(BF16)
            for p in (QUERY, KEY, VALUE):
                product = jnp.dot(scaled, weights[p, core, span(q)], preferred_element_type=F32)
                acc[p, 0] = product if q == 0 else acc[p, 0] + product
        factor = row_factor()
        for p in (QUERY, KEY, VALUE):
            keep(p, core, acc[p, 0] * factor)

    def row_factor():
        return lax.rsqrt(
            jnp.sum(squares[...], axis=1, keepdims=True) * (1.0 / features) + EPS
        )

    def keep(p, side, total):
        if p == QUERY:
            q_unit[side] = unit(total)
        elif p == KEY:
            k_unit[side] = unit(total)
        else:
            v_rows[side] = total.astype(BF16)

    def unit(projected):
        square = projected * projected
        upper = square.astype(BF16)
        lower = (square - upper.astype(F32)).astype(BF16)
        row = lax.broadcasted_iota(jnp.int32, (width, width), 0) // head_size
        column = lax.broadcasted_iota(jnp.int32, (width, width), 1) // head_size
        same = jnp.where(row == column, 1.0 / head_size, 0.0).astype(BF16)
        mean = jnp.dot(upper, same, preferred_element_type=F32) + jnp.dot(
            lower, same, preferred_element_type=F32
        )
        return (projected * lax.rsqrt(mean + EPS)).astype(BF16)

    def attend(side):
        queries = q_unit[side].astype(F32)
        keys = k_unit[side]
        values = v_rows[side]
        lane_head = lax.broadcasted_iota(jnp.int32, (length, width), 1) // head_size
        stacked = jnp.concatenate(
            [jnp.where(lane_head == h, queries, 0.0).astype(BF16) for h in range(heads)], axis=0
        )
        scores = lax.dot_general(
            stacked, keys, (((1,), (1,)), ((), ())), preferred_element_type=F32
        )
        mixture = jnp.zeros((length, width), F32)
        for h in range(heads):
            grown = jnp.exp(scores[h * length : (h + 1) * length] * sharp[side, pl.ds(h, 1)])
            total = jnp.sum(grown, axis=1, keepdims=True)
            share = (grown * (1.0 / total)).astype(BF16)
            mixed = jnp.dot(share, values, preferred_element_type=F32)
            mixture = jnp.where(lane_head == h, mixed, mixture)
        return mixture.astype(BF16)

    def partial(u, i):
        q = chip(*OTHERS[i])
        return remote(
            part_buf.at[q, piece(u)],
            sum_buf.at[here, piece(u)],
            sum_send.at[u, i],
            sum_recv.at[u, here],
            2 * q + core,
        )

    def project_out():
        mixture = [mix_buf[side] for side in range(CORES)]

        def product(q):
            return sum(
                jnp.dot(mixture[side], out_weights[side, :, span(q)], preferred_element_type=F32)
                for side in range(CORES)
            )

        for i, other in enumerate(OTHERS):
            q = chip(*other)
            part_buf[q] = product(q).astype(BF16)
            partial(0, i).start()
        for u in range(1, SUB):
            for i in range(CHIPS - 1):
                partial(u, i).start()
        part_buf[here] = product(here).astype(BF16)

    def onward(u):
        return pltpu.make_async_remote_copy(
            src_ref=own_out.at[piece(u)],
            dst_ref=x_buf.at[here, piece(u)],
            send_sem=next_send.at[u, 0],
            recv_sem=x_recv.at[u, here],
            device_id=(section + 1, me),
            device_id_type=MESH,
        )

    def remember(source, u):
        return pltpu.make_async_remote_copy(
            src_ref=source.at[piece(u)],
            dst_ref=mem_buf.at[here, piece(u)],
            send_sem=next_send.at[u, 1],
            recv_sem=mem_recv.at[u, here],
            device_id=(section + 1, me),
            device_id_type=MESH,
        )

    def share(u, i):
        target = 2 * chip(*OTHERS[i]) + core if i < CHIPS - 1 else partner
        return remote(
            own_out.at[piece(u)],
            cell(core, u, here),
            out_send.at[u, i],
            out_recv.at[core, u, here],
            target,
        )

    def hand(u, i):
        q = chip(*OTHERS[i])
        ref = cell(core, u, q)
        return remote(ref, ref, out_send.at[u, CHIPS + i], out_recv.at[core, u, q], partner)

    def share_begin(u):
        for i in range(CHIPS - 1):
            share(u, i).start()

    def reduce():
        for u in range(SUB):
            at = piece(u)
            total = x_buf[here, at].astype(F32) + part_buf[here, at].astype(F32)
            for other in OTHERS:
                q = chip(*other)
                arrive(sum_buf, sum_recv, u, q)
                total = total + sum_buf[q, at].astype(F32)
            rounded = total.astype(BF16)
            own_out[at] = rounded

            @pl.when((section < sections - 1) & (section != encoders - 1))
            def _():
                onward(u).start()

            @pl.when(section == encoders - 1)
            def _():
                remember(own_out, u).start()

            @pl.when(section == sections - 1)
            def _():
                share(u, CHIPS - 1).start()
                share_begin(u)

            result[0, core, at, span(here)] = rounded

    @pl.when(section == 0)
    def _():
        pltpu.make_async_copy(all_x, all_x, local_sem.at[0]).wait()

    for copy in own_weights:
        copy.wait()

    def local_mixture(m):
        project_local(m)
        mixture = attend(core)

        @pl.when(core == m)
        def _():
            mix_buf[core] = mixture

        @pl.when(core != m)
        def _():
            mix_out[...] = mixture

    pl.when(section == 0)(lambda: local_mixture(0))

    pl.semaphore_wait(barrier, CHIPS + sections - 1)

    @pl.when((section == 0) & (core != 0))
    def _():
        give_mix.start()

    give_out.start()
    give_sharp.start()

    @pl.when(section > 0)
    def _():
        for copy in give:
            copy.start()

    own_out_weights.wait()

    @pl.when(section == 0)
    def _():
        pltpu.make_async_copy(
            inbound.at[core, :, span(here)], x_buf.at[here], local_sem.at[1]
        ).wait()
        give_out.wait_recv()

        @pl.when(core == 0)
        def _():
            landed(mix_buf.at[1 - core], pair_recv.at[5])
            project_out()

        local_mixture(1)

        @pl.when(core == 0)
        def _():
            reduce()
            pl.semaphore_wait(gate, 1)
            give_mix.start()

        @pl.when(core != 0)
        def _():
            landed(mix_buf.at[1 - core], pair_recv.at[5])
            project_out()
            reduce()

        give_sharp.wait_recv()

    @pl.when(section > 0)
    def _():
        give_sharp.wait_recv()
        for copy in give:
            copy.wait_recv()
        everything, context = (QUERY, KEY, VALUE), (KEY, VALUE)

        @pl.when(section == encoders)
        def _():
            pltpu.make_async_copy(x_buf, x_buf, local_sem.at[1]).wait()
            project(x_buf, x_recv, gain, (QUERY,), False)
            enter(mem_buf, mem_recv, mem_send, remember)
            project(mem_buf, mem_recv, last_gain, context, True)

        @pl.when(section > encoders)
        def _():
            enter(mem_buf, mem_recv, mem_send, remember)
            project(mem_buf, mem_recv, last_gain, context, True)
            enter(x_buf, x_recv, x_send)
            project(x_buf, x_recv, gain, (QUERY,), True)

        @pl.when(section < encoders)
        def _():
            enter(x_buf, x_recv, x_send)

            @pl.when((section == 1) & (core == 0))
            def _():
                pl.semaphore_signal(gate, inc=1, device_id=(0, me), device_id_type=MESH)

            project(x_buf, x_recv, gain, everything, True)

        for side in range(CORES):
            mix_buf[side] = attend(side)
        give_out.wait_recv()
        project_out()
        reduce()

    @pl.when(section < sections - 1)
    def _():
        for u in range(SUB):
            pl.when(section != encoders - 1)(lambda: onward(u).wait_send())
            pl.when(section == encoders - 1)(lambda: remember(own_out, u).wait_send())
        for u in range(SUB):
            share(u, CHIPS - 1).start()

    for u in range(SUB):
        landed(cell(1 - core, u, here), out_recv.at[1 - core, u, here])

    @pl.when(section < sections - 1)
    def _():
        for u in range(SUB):
            share_begin(u)

    for u in range(SUB):
        for i, other in enumerate(OTHERS):
            q = chip(*other)
            landed(cell(core, u, q), out_recv.at[core, u, q])
            hand(u, i).start()
    for u in range(SUB):
        for other in OTHERS:
            q = chip(*other)
            landed(cell(1 - core, u, q), out_recv.at[1 - core, u, q])

    give_out.wait_send()
    give_sharp.wait_send()
    pl.when(section == 0)(lambda: give_mix.wait_send())

    @pl.when(section > 0)
    def _():
        for copy in give:
            copy.wait_send()

    for u in range(SUB):
        for i in range(CHIPS - 1):
            partial(u, i).wait_send()
            hand(u, i).wait_send()
        for i in range(CHIPS):
            share(u, i).wait_send()

        @pl.when(section >= encoders)
        def _():
            for copy in spread(mem_buf, mem_recv, mem_send, u):
                copy.wait_send()

        @pl.when((section > 0) & (section != encoders))
        def _():
            for copy in spread(x_buf, x_recv, x_send, u):
                copy.wait_send()

        @pl.when((section >= encoders) & (section < sections - 1))
        def _():
            remember(own_out, u).wait_send()


def solution(mesh):
    sections, seq = mesh.shape["section"], mesh.shape["seq"]

    def shards(inbound, decoder, w_query, w_key, w_value, w_out, gain, sharpness, last_gain):
        batches, length, features = inbound.shape
        width = features // seq
        wide = CORES * width
        dma = pltpu.SemaphoreType.DMA
        blocks = pltpu.VMEM((CHIPS, length, wide), BF16)
        planes = pltpu.VMEM((CORES, length, width), BF16)
        outside = pl.BlockSpec(memory_space=pltpu.HBM)
        vmem = pl.BlockSpec(memory_space=pltpu.VMEM)
        return pl.pallas_call(
            kernel,
            out_shape=jax.ShapeDtypeStruct((1, batches, length, features), BF16),
            in_specs=[outside] * 6 + [vmem, pl.BlockSpec(memory_space=pltpu.SMEM), vmem],
            out_specs=vmem,
            scratch_shapes=[
                pltpu.VMEM((3, CORES, features, width), BF16),
                pltpu.VMEM((CORES, width, features), BF16),
                pltpu.VMEM((batches, CHIPS, length, wide), BF16),
                blocks,
                blocks,
                planes,
                pltpu.VMEM((length, width), BF16),
                blocks,
                blocks,
                pltpu.VMEM((length, wide), BF16),
                pltpu.VMEM((3, CORES, length, width), F32),
                pltpu.VMEM((length, width), F32),
                planes,
                planes,
                planes,
                pltpu.VMEM((CORES, 8, length), F32),
                dma((SUB, CHIPS)),
                dma((SUB, CHIPS)),
                dma((SUB, CHIPS)),
                dma((CORES, SUB, CHIPS)),
                dma((SUB, CHIPS - 1)),
                dma((SUB, CHIPS - 1)),
                dma((SUB, CHIPS - 1)),
                dma((SUB, 2 * CHIPS)),
                dma((SUB, 2)),
                dma((6,)),
                dma((6,)),
                dma((6,)),
                pltpu.SemaphoreType.REGULAR,
            ],
            compiler_params=pltpu.CompilerParams(
                collective_id=0, has_side_effects=True, vmem_limit_bytes=60 * 1024 * 1024
            ),
            name="cascade",
        )(
            inbound,
            decoder,
            w_query,
            w_key,
            w_value,
            w_out,
            gain,
            sharpness,
            last_gain.reshape(1, features),
        )

    return jax.shard_map(
        shards,
        mesh=mesh,
        in_specs=(
            P(),
            P(),
            P("section", None, "seq"),
            P("section", None, "seq"),
            P("section", None, "seq"),
            P("section", "seq", None),
            P("section", None),
            P("section", "seq"),
            P(),
        ),
        out_specs=P("section", None, None, None),
        check_vma=False,
    )
```

time: 1830 us -> 200 us (0.11)
  waiting for transfers between devices: 1600 us -> 0 us
  Pallas kernels: 0 us -> 196 us
  other arithmetic: 91.7 us -> 0 us
  matrix products: 74.6 us -> 0 us
  local copies, waits for them, and re-layouts: 25.1 us -> 3.13 us
    psum x9 -> x0, waiting for transfers between devices: 707 us -> none  [broadcast(): return lax.psum(kept, axis)]
    reduce_scatter x9 -> x0, waiting for transfers between devices: 531 us -> none  [layer(): lax.psum_scatter(jnp.dot(blended_payloads, w_output, preferred_element_ty...]
    all_gather x9 -> x0, waiting for transfers between devices: 358 us -> none  [advance(): outgoing = lax.all_gather(share, 'seq', axis=0, tiled=True)]
    pallas_call x0 -> x1, Pallas kernels: none -> 196 us  [shards(): pl.pallas_call(kernel, out_shape=jax.ShapeDtypeStruct((1, batches, length...]
    dot_general x54 -> x0, matrix products: 74.6 us -> none  [the longest x9 27.4 us: layer(): jnp.dot(blended_payloads, w_output, preferred_element_type=jnp.float32)]
    select_n x27 -> x0, other arithmetic: 32.7 us -> none  [the longest x9 22 us: advance(): finished = jnp.where(valid, written, finished)]
    reduce_sum x9 -> x0, other arithmetic: 25.5 us -> none  [normalize(): jnp.mean(values * values, axis=-1, keepdims=True) + epsilon]
  transfers between devices with their start and end apart: 36 -> 0, of which waited for: 27 -> 0; matrix products, arithmetic and copies ran while one was open for 2% -> 0% of each run, Pallas kernels for 0% -> 0%
where the time goes in v3:
time: 200 us; the launch traced here: 199 us
  Pallas kernels  196 us (98%)
  local copies, waits for them, and re-layouts  3.13 us (2%)
    pallas_call x1, Pallas kernels, shards(): pl.pallas_call(kernel, out_shape=jax.ShapeDtypeStruct((1, batches, length...  196 us

profile of v3, /device:TPU:123, one launch (start us, length us, event | category | flops | bytes accessed | tf_op | source)
XLA Modules:
  0.0 199.0 jit_solution(411825229231340158)
XLA Ops:
  0.0 195.8 %cascade.1 = bf16[1,2,128,4096]{3,2,1,0:T(8,128)(2,1)} custom-call(bf16[2,128,4096]{2,1,0:T(8,128)(2,1)} %inbound.1, bf16[2,128,4096]{2,1,0:T(8,128)(2,1)} %decoder.1, bf16[1,4096,256]{2,1,0:T(8,128)(2,1)} %w_query.1, bf16[1,4096,256]{2,1,0:T(8,128)(2,1)} %w_key.1, bf16[1,4096,256]{2,1,0:T(8,128)(2,1)} %w_value.1, bf16[1,256,4096]{2,1,0:T(8,128)(2,1)} %w_out.1, ...), custom_call_target="tpu_custom_call" | custom-call | tf_op jit(solution)/shard_map/cascade/pallas_call | solution.py:526
  195.9 3.1 %copy.11 = bf16[1,2,128,4096]{3,2,1,0:T(8,128)(2,1)} copy(bf16[1,2,128,4096]{3,2,1,0:T(8,128)(2,1)} %cascade.1) | data formatting | bytes 4194304

commit v4 on v3

--- a/solution.py
+++ b/solution.py
@@ -14,7 +14,7 @@
 CHIPS = 2 * RING
 CORES = 2
 OTHERS = ((2, 1), (1, 1), (-1, 1), (2, 0), (0, 1), (1, 0), (-1, 0))
-SUB = 8
+SUB = 4
 
 QUERY, KEY, VALUE = 0, 1, 2
 
@@ -58,7 +58,6 @@
     local_sem,
     pair_recv,
     pair_send,
-    gate,
 ):
     sections = lax.axis_size("section")
     encoders = 3 * sections // 8
@@ -170,11 +169,9 @@
     def arrive(buf, recv, u, q):
         landed(buf.at[q, piece(u)], recv.at[u, q])
 
-    def enter(buf, recv, send, ahead=None):
+    def enter(buf, recv, send):
         for u in range(SUB):
             arrive(buf, recv, u, here)
-            if ahead is not None:
-                pl.when(section < sections - 1)(lambda: ahead(buf.at[here], u).start())
             for copy in spread(buf, recv, send, u):
                 copy.start()
 
@@ -297,13 +294,13 @@
             device_id_type=MESH,
         )
 
-    def remember(source, u):
+    def to_memory(u, i):
         return pltpu.make_async_remote_copy(
-            src_ref=source.at[piece(u)],
+            src_ref=own_out.at[piece(u)],
             dst_ref=mem_buf.at[here, piece(u)],
-            send_sem=next_send.at[u, 1],
+            send_sem=next_send.at[u, i],
             recv_sem=mem_recv.at[u, here],
-            device_id=(section + 1, me),
+            device_id=(encoders + i, me),
             device_id_type=MESH,
         )
 
@@ -323,7 +320,7 @@
         return remote(ref, ref, out_send.at[u, CHIPS + i], out_recv.at[core, u, q], partner)
 
     def share_begin(u):
-        for i in range(CHIPS - 1):
+        for i in range(CHIPS):
             share(u, i).start()
 
     def reduce():
@@ -343,11 +340,11 @@
 
             @pl.when(section == encoders - 1)
             def _():
-                remember(own_out, u).start()
+                for i in range(sections - encoders):
+                    to_memory(u, i).start()
 
             @pl.when(section == sections - 1)
             def _():
-                share(u, CHIPS - 1).start()
                 share_begin(u)
 
             result[0, core, at, span(here)] = rounded
@@ -406,12 +403,12 @@
         @pl.when(core == 0)
         def _():
             reduce()
-            pl.semaphore_wait(gate, 1)
             give_mix.start()
 
         @pl.when(core != 0)
         def _():
             landed(mix_buf.at[1 - core], pair_recv.at[5])
+            pl.delay(13000)
             project_out()
             reduce()
 
@@ -428,12 +425,12 @@
         def _():
             pltpu.make_async_copy(x_buf, x_buf, local_sem.at[1]).wait()
             project(x_buf, x_recv, gain, (QUERY,), False)
-            enter(mem_buf, mem_recv, mem_send, remember)
+            enter(mem_buf, mem_recv, mem_send)
             project(mem_buf, mem_recv, last_gain, context, True)
 
         @pl.when(section > encoders)
         def _():
-            enter(mem_buf, mem_recv, mem_send, remember)
+            enter(mem_buf, mem_recv, mem_send)
             project(mem_buf, mem_recv, last_gain, context, True)
             enter(x_buf, x_recv, x_send)
             project(x_buf, x_recv, gain, (QUERY,), True)
@@ -441,11 +438,6 @@
         @pl.when(section < encoders)
         def _():
             enter(x_buf, x_recv, x_send)
-
-            @pl.when((section == 1) & (core == 0))
-            def _():
-                pl.semaphore_signal(gate, inc=1, device_id=(0, me), device_id_type=MESH)
-
             project(x_buf, x_recv, gain, everything, True)
 
         for side in range(CORES):
@@ -453,17 +445,6 @@
         give_out.wait_recv()
         project_out()
         reduce()
-
-    @pl.when(section < sections - 1)
-    def _():
-        for u in range(SUB):
-            pl.when(section != encoders - 1)(lambda: onward(u).wait_send())
-            pl.when(section == encoders - 1)(lambda: remember(own_out, u).wait_send())
-        for u in range(SUB):
-            share(u, CHIPS - 1).start()
-
-    for u in range(SUB):
-        landed(cell(1 - core, u, here), out_recv.at[1 - core, u, here])
 
     @pl.when(section < sections - 1)
     def _():
@@ -476,7 +457,7 @@
             landed(cell(core, u, q), out_recv.at[core, u, q])
             hand(u, i).start()
     for u in range(SUB):
-        for other in OTHERS:
+        for other in ((0, 0),) + OTHERS:
             q = chip(*other)
             landed(cell(1 - core, u, q), out_recv.at[1 - core, u, q])
 
@@ -506,9 +487,14 @@
             for copy in spread(x_buf, x_recv, x_send, u):
                 copy.wait_send()
 
-        @pl.when((section >= encoders) & (section < sections - 1))
-        def _():
-            remember(own_out, u).wait_send()
+        @pl.when((section < sections - 1) & (section != encoders - 1))
+        def _():
+            onward(u).wait_send()
+
+        @pl.when(section == encoders - 1)
+        def _():
+            for i in range(sections - encoders):
+                to_memory(u, i).wait_send()
 
 
 def solution(mesh):
@@ -553,11 +539,10 @@
                 dma((SUB, CHIPS - 1)),
                 dma((SUB, CHIPS - 1)),
                 dma((SUB, 2 * CHIPS)),
-                dma((SUB, 2)),
+                dma((SUB, sections)),
                 dma((6,)),
                 dma((6,)),
                 dma((6,)),
-                pltpu.SemaphoreType.REGULAR,
             ],
             compiler_params=pltpu.CompilerParams(
                 collective_id=0, has_side_effects=True, vmem_limit_bytes=60 * 1024 * 1024

time: 200 us -> 194 us (0.970)
  Pallas kernels: 196 us -> 190 us
    pallas_call x1, Pallas kernels: 196 us -> 190 us  [shards(): pl.pallas_call(kernel, out_shape=jax.ShapeDtypeStruct((1, batches, length...]
where the time goes in v4:
time: 194 us; the launch traced here: 193 us
  Pallas kernels  190 us (98%)
  local copies, waits for them, and re-layouts  3.13 us (2%)
    pallas_call x1, Pallas kernels, shards(): pl.pallas_call(kernel, out_shape=jax.ShapeDtypeStruct((1, batches, length...  190 us

profile of v4, /device:TPU:123, one launch (start us, length us, event | category | flops | bytes accessed | tf_op | source)
XLA Modules:
  0.0 193.2 jit_solution(6572812087835922642)
XLA Ops:
  0.0 190.1 %cascade.1 = bf16[1,2,128,4096]{3,2,1,0:T(8,128)(2,1)} custom-call(bf16[2,128,4096]{2,1,0:T(8,128)(2,1)} %inbound.1, bf16[2,128,4096]{2,1,0:T(8,128)(2,1)} %decoder.1, bf16[1,4096,256]{2,1,0:T(8,128)(2,1)} %w_query.1, bf16[1,4096,256]{2,1,0:T(8,128)(2,1)} %w_key.1, bf16[1,4096,256]{2,1,0:T(8,128)(2,1)} %w_value.1, bf16[1,256,4096]{2,1,0:T(8,128)(2,1)} %w_out.1, ...), custom_call_target="tpu_custom_call" | custom-call | tf_op jit(solution)/shard_map/cascade/pallas_call | solution.py:512
  190.1 3.1 %copy.11 = bf16[1,2,128,4096]{3,2,1,0:T(8,128)(2,1)} copy(bf16[1,2,128,4096]{3,2,1,0:T(8,128)(2,1)} %cascade.1) | data formatting | bytes 4194304
